TPU v7x, 256 devices: a whole 4x4x8 slice. The times are simulated.
256 devices in a mesh: req: 16 (over y, z_lo, core), blk: 16 (over z_hi, x).
Axes of the slice: x: 4, y: 4, z: 8 (z_hi: 4, z_lo: 2; z = z_hi * 2 + z_lo), core: 2. Of those that a mesh axis runs over, the one named last changes fastest.
Arguments:
- queries: bfloat16 [2048, 8192], P('req', 'blk'), may hold values from -120 to 120
- suffix_key_value: bfloat16 [2048, 8, 256], P('req'), may hold values from -6 to 6
- residual: bfloat16 [2048, 8192], P('req', 'blk'), may hold values from -10 to 10
- gain: float32 [8192], P('blk'), may hold values from 0.1 to 1.9
- gate_up: bfloat16 [8192, 2, 14336], P('blk', None, 'req'), may hold values from -0.0625 to 0.0625
- prefix_cache_slots: bfloat16 [128, 128, 8, 256], P('req'), may hold values from -6 to 6
- prefix_page_slots: int32 [128], replicated, may hold values from 0 to 127, each once
- lengths: int32 [16, 4], replicated, may hold values from 1 to 64, 128 in all within a row
- counts: int32 [16], replicated, may hold values from 1 to 128, as said below
Outputs:
- hidden: bfloat16 [2048, 14336], P('blk', 'req')
- suffix_cache: bfloat16 [2048, 2048], P('req', 'blk')
Inputs may be any that keep to these rules, and one draw needn't show every extreme that they name: `prefix_page_slots`: slot s of prefix_cache_slots lies on index s // 8 of req; every slot holds exactly one page. Each group's lengths sum to 128, and each group has one request of exactly 64 tokens. `counts`: some group reads all 128 pages.
All inputs are finite; a program needn't handle non-finite values.
Results may differ from a plain program's by a relative error of at most 0.034.
Values may be sent and summed in bfloat16 or wider, within the bound.
A program may use at most 256 MiB of HBM per device.

v0:
```python
import math

import jax
import jax.numpy as jnp
from jax import lax
from jax.sharding import PartitionSpec as P

D = 8192


NEGATIVE = -1e30
EPSILON = 1e-05
ROPE_BASE = 500000.0


def rope_tables(positions, half_dim):
    inverse = jnp.exp(
        -math.log(ROPE_BASE) * jnp.arange(half_dim, dtype=jnp.float32) * 2.0 / (2 * half_dim)
    )
    angles = positions.astype(jnp.float32)[:, None] * inverse[None, :]
    return (jnp.cos(angles), jnp.sin(angles))


def rotate(vectors, cosines, sines):
    half_dim = vectors.shape[-1] // 2
    lower = vectors[..., :half_dim]
    upper = vectors[..., half_dim:]
    return jnp.concatenate([lower * cosines - upper * sines, upper * cosines + lower * sines], -1)


def suffix_layout(lengths_row, page_count, group_len, page_len):
    starts = jnp.cumsum(lengths_row) - lengths_row
    tokens_at = jnp.arange(group_len, dtype=jnp.int32)
    request = jnp.sum((tokens_at[:, None] >= starts[None, :]).astype(jnp.int32), 1) - 1
    slots_req = jnp.arange(lengths_row.shape[0], dtype=jnp.int32)
    request_begin = jnp.sum(
        jnp.where(request[:, None] == slots_req[None, :], starts[None, :], 0), 1
    )
    offset = tokens_at - request_begin
    return (request, offset, page_count * page_len + offset)


def absorb(state, query, keys_in, values_in, usable, score_scale):
    weighted, running_max, weight_sum = state
    scores = (
        jnp.einsum("tqd,nd->tqn", query, keys_in, preferred_element_type=jnp.float32) * score_scale
    )
    scores = jnp.where(usable, scores, NEGATIVE)
    new_max = jnp.maximum(running_max, jnp.max(scores, -1))
    probs = jnp.where(usable, jnp.exp(scores - new_max[..., None]), 0.0)
    factor = jnp.exp(running_max - new_max)
    weight_sum = weight_sum * factor + jnp.sum(probs, -1)
    weighted = weighted * factor[..., None] + jnp.einsum(
        "tqn,nd->tqd", probs.astype(jnp.bfloat16), values_in, preferred_element_type=jnp.float32
    )
    return (weighted, new_max, weight_sum)


def absorb_pages(state, query, pages_in, page_numbers, limit, score_scale):
    n_pages, page_len, lanes = pages_in.shape
    head_dim = lanes // 2
    key_target = max(page_len, (1 << 20) // (query.shape[0] * query.shape[1]))
    per_block = math.gcd(n_pages, max(1, key_target // page_len))
    n_blocks = n_pages // per_block

    def step(index, carry):
        block = lax.dynamic_slice_in_dim(pages_in, index * per_block, per_block, 0).reshape(
            per_block * page_len, lanes
        )
        numbers = lax.dynamic_slice_in_dim(page_numbers, index * per_block, per_block, 0)
        usable = jnp.repeat(numbers, page_len)[None, None, :] < limit
        return absorb(carry, query, block[:, :head_dim], block[:, head_dim:], usable, score_scale)

    return lax.fori_loop(0, n_blocks, step, state)


def empty_state(rows_count, heads_here, head_dim):
    return (
        jnp.zeros((rows_count, heads_here, head_dim), jnp.float32),
        jnp.full((rows_count, heads_here), NEGATIVE, jnp.float32),
        jnp.zeros((rows_count, heads_here), jnp.float32),
    )


def on_device(
    queries,
    suffix_key_value,
    residual,
    gain,
    gate_up,
    prefix_cache_slots,
    prefix_page_slots,
    lengths,
    counts,
):
    blocks = lax.axis_size("blk")
    column = lax.axis_index("blk")
    group_index = lax.axis_index("req")
    group_len = queries.shape[0]
    heads_kv = suffix_key_value.shape[1]
    head_dim = suffix_key_value.shape[2] // 2
    heads_here = queries.shape[1] // head_dim
    page_len = prefix_cache_slots.shape[1]
    score_scale = 1.0 / math.sqrt(head_dim)
    kv_head = column * heads_kv // blocks
    page_count = counts[group_index]
    request, offset, positions = suffix_layout(
        lengths[group_index], page_count, group_len, page_len
    )
    cosines, sines = rope_tables(positions, head_dim // 2)
    rotated_query = rotate(
        queries.astype(jnp.float32).reshape(group_len, heads_here, head_dim),
        cosines[:, None],
        sines[:, None],
    ).astype(jnp.bfloat16)
    own_head = lax.dynamic_index_in_dim(suffix_key_value, kv_head, 1, keepdims=False)
    keys_new = rotate(own_head[:, :head_dim].astype(jnp.float32), cosines, sines).astype(
        jnp.bfloat16
    )
    values_new = own_head[:, head_dim:]
    both_new = jnp.concatenate([keys_new, values_new], 1)
    lane_width = 2 * heads_kv * head_dim // blocks
    updated_cache = lax.dynamic_slice_in_dim(
        both_new, column * lane_width % (2 * head_dim), lane_width, 1
    )
    allowed = (request[:, None] == request[None, :]) & (offset[None, :] <= offset[:, None])
    state = absorb(
        empty_state(group_len, heads_here, head_dim),
        rotated_query,
        keys_new,
        values_new,
        allowed[:, None, :],
        score_scale,
    )
    pages_total = prefix_page_slots.shape[0]
    page_ids = jnp.arange(pages_total, dtype=jnp.int32)
    own_slots = lax.dynamic_index_in_dim(prefix_cache_slots, kv_head, 2, keepdims=False)
    shard_piece = lax.all_gather(own_slots, "req", axis=0, tiled=True)
    slot_ids = jnp.arange(shard_piece.shape[0], dtype=jnp.int32)
    match = prefix_page_slots[None, :] == slot_ids[:, None]
    state = absorb_pages(
        state,
        rotated_query,
        shard_piece,
        jnp.sum(jnp.where(match, page_ids[None, :], 0), 1),
        page_count,
        score_scale,
    )
    attention_output = (state[0] / state[2][..., None]).reshape(group_len, heads_here * head_dim)
    stream = (residual.astype(jnp.float32) + attention_output).astype(jnp.bfloat16)
    stream_f32 = stream.astype(jnp.float32)
    square_sum = lax.psum(jnp.sum(stream_f32 * stream_f32, 1), "blk")
    normed = (stream_f32 * lax.rsqrt(square_sum[:, None] / D + EPSILON) * gain[None, :]).astype(
        jnp.bfloat16
    )
    gathered = lax.all_gather(normed, "req", axis=0, tiled=True)
    weights = gate_up.reshape(gate_up.shape[0], 2 * gate_up.shape[2])
    width_here = gate_up.shape[2]
    summed = lax.psum_scatter(
        jnp.dot(gathered, weights, preferred_element_type=jnp.float32).astype(jnp.bfloat16),
        "blk",
        scatter_dimension=0,
        tiled=True,
    ).astype(jnp.float32)
    hidden = (jax.nn.silu(summed[:, :width_here]) * summed[:, width_here:]).astype(jnp.bfloat16)
    return (hidden, updated_cache)


def solution(mesh):
    placed = (
        P("req", "blk"),
        P("req", None, None),
        P("req", "blk"),
        P("blk"),
        P("blk", None, "req"),
        P("req", None, None, None),
        P(),
        P(),
        P(),
    )
    return jax.shard_map(
        on_device,
        mesh=mesh,
        in_specs=placed,
        out_specs=(P("blk", "req"), P("req", "blk")),
        check_vma=False,
    )
```

profile of v0, /device:TPU:20, one launch (start us, length us, event | category | flops | bytes accessed | tf_op | source)
XLA Modules:
  0.0 334.2 jit_solution(3591659138947527602)
XLA Ops:
  7.3 3.4 %constant_dynamic-slice_fusion.1 = bf16[8,128,1,256]{3,2,1,0:T(2,128)(2,1)S(1)} fusion(bf16[8,128,8,256]{3,2,1,0:T(8,128)(2,1)} %param.16, s32[]{:T(128)S(6)} %select_n.68), kind=kLoop, calls=%fused_computation.69 | loop fusion | bytes 1048580 | tf_op jit(solution)/shard_map/jit(dynamic_index_in_dim)/dynamic_slice | solution.py:137
  15.5 53.3 %all-gather.6.cloned.1.call-done = bf16[128,128,1,256]{3,1,2,0:T(8,128)(2,1)} async-done(((bf16[8,128,1,256]{3,1,2,0:T(8,128)(2,1)}), bf16[128,128,1,256]{3,1,2,0:T(8,128)(2,1)}) %all-gather.6.cloned.1.call-update) | async-done | bytes 8388624 | tf_op jit(solution)/shard_map/all_gather | solution.py:138
  68.8 51.6 %while.17 = (s32[]{:T(128)}, f32[128,4,128]{2,0,1:T(8,128)S(1)}, f32[128,4]{0,1:T(4,128)S(1)}, f32[128,4]{0,1:T(4,128)S(1)}, s32[128]{0:T(128)S(1)}, /*index=5*/...) while((s32[]{:T(128)}, f32[128,4,128]{2,0,1:T(8,128)S(1)}, ...), condition=%wide.region_9.10_spmd, body=%wide.region_6.9_spmd.sunk | while | flops 550634496 | bytes 16427279 | solution.py:74
  71.9 1.6 fusion.49
  73.5 1.9 fusion.50
  78.3 1.6 fusion.49
  79.9 1.9 fusion.50
  84.7 1.6 fusion.49
  86.4 1.9 fusion.50
  91.2 1.6 fusion.49
  92.8 1.9 fusion.50
  97.6 1.6 fusion.49
  99.2 1.9 fusion.50
  104.1 1.6 fusion.49
  105.7 1.9 fusion.50
  110.5 1.6 fusion.49
  112.1 1.9 fusion.50
  116.9 1.6 fusion.49
  118.5 1.9 fusion.50
  120.7 40.2 %psum.7 = f32[128]{0:T(128)S(1)} all-reduce(f32[128]{0:T(128)S(1)} %fusion.17), channel_id=1, replica_groups=mesh['req'=16,'blk'=16] {'blk'}, use_global_device_ids=true, to_apply=%region_11.12 | all-reduce | flops 128 | bytes 1024 | tf_op jit(solution)/shard_map/psum | solution.py:152
  161.8 1.5 copy.47
  163.3 38.1 %all-gather.4.cloned.1.call-done = bf16[2048,512]{0,1:T(8,128)(2,1)} async-done(((bf16[128,512]{0,1:T(8,128)(2,1)}), bf16[2048,512]{0,1:T(8,128)(2,1)}) %all-gather.4.cloned.1.call-update) | async-done | bytes 2097168 | tf_op jit(solution)/shard_map/all_gather | solution.py:156
  201.4 9.1 %convolution_convert_fusion = bf16[2048,1792]{1,0:T(8,128)(2,1)} fusion(bf16[2048,512]{0,1:T(8,128)(2,1)} %all-gather.4.cloned.1.call-done, bf16[512,1792]{1,0:T(8,128)(2,1)} %bitcast.74), kind=kOutput, calls=%fused_computation.22 | convolution fusion | flops 3761766400 | bytes 11272192 | tf_op jit(solution)/shard_map/dot_general | solution.py:160
  211.3 114.5 %reduce-scatter.2.cloned.1.call-done = bf16[128,1792]{1,0:T(8,128)(2,1)} async-done(((bf16[2048,1792]{1,0:T(8,128)(2,1)}), bf16[128,1792]{1,0:T(8,128)(2,1)}) %reduce-scatter.2.cloned.1.call-update) | async-done | bytes 458768 | tf_op jit(solution)/shard_map/reduce_scatter | solution.py:159
  (114 shorter events, 31.0 us)
Async XLA Ops:
  7.2 4.5 %copy-start = (bf16[128,8,256]{2,1,0:T(8,128)(2,1)S(1)}, bf16[128,8,256]{2,1,0:T(8,128)(2,1)}, u32[]{:S(2)}) copy-start(bf16[128,8,256]{2,1,0:T(8,128)(2,1)} %param.12) | copy-start | bytes 1572868
  7.2 4.7 %copy-start.4 = (s32[16,4]{0,1:T(4,128)S(1)}, s32[16,4]{0,1:T(4,128)}, u32[]{:S(2)}) copy-start(s32[16,4]{0,1:T(4,128)} %param.18) | copy-start | bytes 772
  7.2 4.8 %copy-start.6 = (s32[16]{0:T(128)S(1)}, s32[16]{0:T(128)}, u32[]{:S(2)}) copy-start(s32[16]{0:T(128)} %param.19) | copy-start | bytes 196
  7.2 5.4 %copy-start.2 = (bf16[128,512]{1,0:T(8,128)(2,1)S(1)}, bf16[128,512]{1,0:T(8,128)(2,1)}, u32[]{:S(2)}) copy-start(bf16[128,512]{1,0:T(8,128)(2,1)} %param.11) | copy-start | bytes 393220
  7.2 5.8 %copy-start.3 = (bf16[128,512]{1,0:T(8,128)(2,1)S(1)}, bf16[128,512]{1,0:T(8,128)(2,1)}, u32[]{:S(2)}) copy-start(bf16[128,512]{1,0:T(8,128)(2,1)} %param.13) | copy-start | bytes 393220
  7.2 6.9 %copy-start.7 = (s32[128]{0:T(128)S(1)}, s32[128]{0:T(128)}, u32[]{:S(2)}) copy-start(s32[128]{0:T(128)} %param.17) | copy-start | bytes 1540
  7.2 61.6 %all-gather.6.cloned.1.call-start = ((), (), s32[]{:S(2)}) async-start(), calls=%async_computation.3 | async-start | bytes 8912896 | tf_op jit(solution)/shard_map/all_gather | solution.py:138
  11.6 189.7 %all-gather.4.cloned.1.call-start = ((), (), s32[]{:S(2)}) async-start(), calls=%async_computation.1 | async-start | bytes 2228224 | tf_op jit(solution)/shard_map/all_gather | solution.py:156
  68.8 92.1 %copy-start.5 = (f32[512]{0:T(512)S(1)}, f32[512]{0:T(512)}, u32[]{:S(2)}) copy-start(f32[512]{0:T(512)} %param.14) | copy-start | bytes 6148
  68.8 92.9 %copy-start.1 = (bf16[512,2,896]{2,1,0:T(2,128)(2,1)S(1)}, bf16[512,2,896]{2,1,0:T(2,128)(2,1)}, u32[]{:S(2)}) copy-start(bf16[512,2,896]{2,1,0:T(2,128)(2,1)} %param.15) | copy-start | bytes 5505028
  161.7 164.0 %reduce-scatter.2.cloned.1.call-start = ((), (), s32[]{:S(2)}) async-start(), calls=%async_computation.2 | async-start | bytes 7798784 | tf_op jit(solution)/shard_map/reduce_scatter | solution.py:159
Sparse Core Ops, SparseCore 0:
  11.8 57.0 all-gather.5
  161.8 39.4 all-gather.3
  210.6 115.0 reduce-scatter.1
where the time goes:
time: 335 us; the launch traced here: 334 us
  waiting for transfers between devices  206 us (61%)
  blocking collectives  40.2 us (12%)
  matrix products  30.8 us (9%)
  other arithmetic  23.6 us (7%)
  local copies, waits for them, and re-layouts  18.4 us (5%)
  between operations  14.7 us (4%)
    reduce_scatter x1, waiting for transfers between devices, on_device(): lax.psum_scatter(jnp.dot(gathered, weights, preferred_element_type=jnp.fl...  114 us
    all_gather x1, waiting for transfers between devices, on_device(): shard_piece = lax.all_gather(own_slots, 'req', axis=0, tiled=True)  53.3 us
    psum x1, blocking collectives, on_device(): square_sum = lax.psum(jnp.sum(stream_f32 * stream_f32, 1), 'blk')  40.2 us
    all_gather x1, waiting for transfers between devices, on_device(): gathered = lax.all_gather(normed, 'req', axis=0, tiled=True)  38.1 us
    dot_general x9, matrix products, absorb(): jnp.einsum('tqn,nd->tqd', probs.astype(jnp.bfloat16), values_in, preferre...  15.4 us
    reduce_sum x9, other arithmetic, absorb(): weight_sum = weight_sum * factor + jnp.sum(probs, -1)  12.9 us
    dynamic_slice x8, local copies, waits for them, and re-layouts, step(): lax.dynamic_slice_in_dim(pages_in, index * per_block, per_block, 0)  10.5 us
    dot_general x1, matrix products, on_device(): jnp.dot(gathered, weights, preferred_element_type=jnp.float32)  9.12 us
  transfers between devices with their start and end apart: 3, of which 3 were waited for; matrix products, arithmetic and copies ran while one was open for 2% of the time, Pallas kernels for 0%

commit v1 on v0

--- a/solution.py
+++ b/solution.py
@@ -3,9 +3,13 @@
 import jax
 import jax.numpy as jnp
 from jax import lax
+from jax.experimental import pallas as pl
+from jax.experimental.pallas import tpu as pltpu
 from jax.sharding import PartitionSpec as P
 
 D = 8192
+
+MESH = pl.DeviceIdType.MESH
 
 
 NEGATIVE = -1e30
@@ -80,6 +84,432 @@
         jnp.full((rows_count, heads_here), NEGATIVE, jnp.float32),
         jnp.zeros((rows_count, heads_here), jnp.float32),
     )
+
+
+def remote(src, dst, send_sem, recv_sem, req, blk):
+    return pltpu.make_async_remote_copy(
+        src_ref=src,
+        dst_ref=dst,
+        send_sem=send_sem,
+        recv_sem=recv_sem,
+        device_id=(req, blk),
+        device_id_type=MESH,
+    )
+
+
+def place():
+    req, blk = lax.axis_index("req"), lax.axis_index("blk")
+    y, zl, core = req // 4, (req // 2) % 2, req % 2
+    return req, blk, y, zl, core, blk // 4, blk % 4
+
+
+def weight_sends(w_ref, w_all, send, recv):
+    req, blk, y, zl, core, zh, x = place()
+    half = w_ref.shape[0] // 2
+    out = []
+    for j, (step, part) in enumerate(((1, 0), (-1, 1), (1, 1), (-1, 0))):
+        rows = pl.ds(part * half, half)
+        out.append(
+            remote(
+                w_ref.at[rows],
+                w_all.at[x, rows],
+                send.at[j],
+                recv.at[x, part],
+                req,
+                zh * 4 + (x + 4 + step) % 4,
+            )
+        )
+    return out
+
+
+def weight_relays(w_all, send, recv):
+    req, blk, y, zl, core, zh, x = place()
+    half = w_all.shape[1] // 2
+    out = []
+    for j, (step, part) in enumerate(((1, 0), (-1, 1))):
+        source = (x + 4 - step) % 4
+        rows = pl.ds(part * half, half)
+        piece = w_all.at[source, rows]
+        out.append(
+            remote(
+                piece,
+                piece,
+                send.at[4 + j],
+                recv.at[source, part],
+                req,
+                zh * 4 + (x + 4 + step) % 4,
+            )
+        )
+    return out
+
+
+def weight_wait(w_all, send, recv, source, part):
+    req, blk, y, zl, core, zh, x = place()
+    half = w_all.shape[1] // 2
+    piece = w_all.at[source, pl.ds(part * half, half)]
+    remote(piece, piece, send.at[0], recv.at[source, part], req, zh * 4 + (x + 1) % 4).wait_recv()
+
+
+def spread_features(u_ref, a_all, x_send, z_send, y_send, on_send, core_send, recv):
+    req, blk, y, zl, core, zh, x = place()
+    target = zl * 2 + core
+    home = core == x % 2
+    root = x == target
+    over_z = y * 4 + (1 - zl) * 2 + core
+    sibling = y * 4 + zl * 2 + (1 - core)
+    up, down = (y + 1) % 4, (y + 3) % 4
+    far = (y + 2) % 4
+    req_up, req_down = up * 4 + zl * 2 + core, down * 4 + zl * 2 + core
+
+    def block_copy(yy, xx, send, to_req, to_blk):
+        piece = a_all.at[yy, xx]
+        return remote(piece, piece, send, recv.at[yy, xx], to_req, to_blk)
+
+    hop = remote(u_ref, a_all.at[y, x], x_send, recv.at[y, x], req, zh * 4 + target)
+    keep = pltpu.make_async_copy(u_ref, a_all.at[y, x], recv.at[y, x])
+
+    @pl.when(root)
+    def _():
+        keep.start()
+
+    @pl.when(jnp.logical_not(root))
+    def _():
+        hop.start()
+
+    def to_core(yy, xx):
+        return block_copy(yy, xx, core_send.at[yy, xx], sibling, blk)
+
+    def to_z(xx):
+        return block_copy(y, xx, z_send.at[xx], over_z, blk)
+
+    def to_y(xx, way):
+        return block_copy(y, xx, y_send.at[xx, way], (req_up, req_down)[way], blk)
+
+    def onward(xx, way):
+        return block_copy((down, up)[way], xx, on_send.at[xx], (req_up, req_down)[way], blk)
+
+    def arrived(yy, xx):
+        block_copy(yy, xx, x_send, over_z, blk).wait_recv()
+
+    @pl.when(home)
+    def _():
+        def own(xx, carry):
+            @pl.when(root & (xx == x))
+            def _():
+                keep.wait()
+
+            @pl.when(jnp.logical_not(root & (xx == x)))
+            def _():
+                arrived(y, xx)
+
+            @pl.when(root)
+            def _():
+                to_z(xx).start()
+
+            to_y(xx, 0).start()
+            to_y(xx, 1).start()
+            to_core(y, xx).start()
+            return carry
+
+        lax.fori_loop(0, 4, own, 0)
+
+        def near(xx, carry):
+            arrived(down, xx)
+
+            @pl.when(xx < 2)
+            def _():
+                onward(xx, 0).start()
+
+            to_core(down, xx).start()
+            arrived(up, xx)
+
+            @pl.when(xx >= 2)
+            def _():
+                onward(xx, 1).start()
+
+            to_core(up, xx).start()
+            return carry
+
+        lax.fori_loop(0, 4, near, 0)
+
+        def last(xx, carry):
+            arrived(far, xx)
+            to_core(far, xx).start()
+            return carry
+
+        lax.fori_loop(0, 4, last, 0)
+
+    @pl.when(jnp.logical_not(home))
+    def _():
+        def take(i, carry):
+            arrived(i // 4, i % 4)
+            return carry
+
+        lax.fori_loop(0, 16, take, 0)
+
+    def drain():
+        @pl.when(jnp.logical_not(root))
+        def _():
+            hop.wait_send()
+
+        @pl.when(home)
+        def _():
+            def step(xx, carry):
+                @pl.when(root)
+                def _():
+                    to_z(xx).wait_send()
+
+                to_y(xx, 0).wait_send()
+                to_y(xx, 1).wait_send()
+
+                @pl.when(xx < 2)
+                def _():
+                    onward(xx, 0).wait_send()
+
+                @pl.when(xx >= 2)
+                def _():
+                    onward(xx, 1).wait_send()
+
+                return carry
+
+            lax.fori_loop(0, 4, step, 0)
+
+            def core_step(i, carry):
+                to_core(i // 4, i % 4).wait_send()
+                return carry
+
+            lax.fori_loop(0, 16, core_step, 0)
+
+    return drain
+
+
+def ffn_kernel(
+    u_ref,
+    w_ref,
+    hidden_ref,
+    w_all,
+    a_all,
+    product,
+    relay,
+    final,
+    own_sum,
+    square_out,
+    square_in,
+    w_send,
+    w_recv,
+    w_local,
+    x_send,
+    z_send,
+    y_send,
+    on_send,
+    core_send,
+    a_recv,
+    r_send,
+    relay_recv,
+    final_recv,
+    q_send,
+    q_recv,
+):
+    req, blk, y, zl, core, zh, x = place()
+    tokens, features = 128, u_ref.shape[1]
+    width = hidden_ref.shape[1]
+    tiles = 2 * width // 256
+    over_z = y * 4 + (1 - zl) * 2 + core
+    sibling = y * 4 + zl * 2 + (1 - core)
+    req_up = ((y + 1) % 4) * 4 + zl * 2 + core
+    req_down = ((y + 3) % 4) * 4 + zl * 2 + core
+    blk_up, blk_far, blk_down = [((zh + i) % 4) * 4 + x for i in (1, 2, 3)]
+
+    barrier = pltpu.get_barrier_semaphore()
+    peers = [(req, zh * 4 + (x + i) % 4) for i in (1, 2, 3)]
+    peers += [(over_z, blk), (sibling, blk), (req_up, blk), (req_down, blk)]
+    peers += [(req, blk_up), (req, blk_far), (req, blk_down)]
+    for peer in peers:
+        pl.semaphore_signal(barrier, inc=1, device_id=peer, device_id_type=MESH)
+    pl.semaphore_wait(barrier, len(peers))
+
+    sends = weight_sends(w_ref, w_all, w_send, w_recv)
+    for copy in sends:
+        copy.start()
+    local = pltpu.make_async_copy(w_ref, w_all.at[x], w_local)
+    local.start()
+
+    drain = spread_features(u_ref, a_all, x_send, z_send, y_send, on_send, core_send, a_recv)
+
+    relays = weight_relays(w_all, w_send, w_recv)
+    for (step, part), copy in zip(((1, 0), (-1, 1)), relays):
+        weight_wait(w_all, w_send, w_recv, (x + 4 - step) % 4, part)
+        copy.start()
+
+    def squares(zt, carry):
+        total = jnp.zeros((8, 128), jnp.float32)
+        for xx in range(4):
+            rows = a_all[zt, xx, tokens : tokens + 16, 0:256].astype(jnp.float32)
+            total = total + rows[0:8, 0:128] + rows[0:8, 128:256]
+        square_out[zt] = total
+        return carry
+
+    lax.fori_loop(0, 4, squares, 0)
+    square_copies = []
+    for i in (1, 2, 3):
+        there = (zh + i) % 4
+        square_copies.append(
+            remote(
+                square_out.at[there],
+                square_in.at[i - 1],
+                q_send.at[i - 1],
+                q_recv.at[i - 1],
+                req,
+                there * 4 + x,
+            )
+        )
+    for copy in square_copies:
+        copy.start()
+
+    weight_wait(w_all, w_send, w_recv, (x + 3) % 4, 1)
+    weight_wait(w_all, w_send, w_recv, (x + 1) % 4, 0)
+    weight_wait(w_all, w_send, w_recv, (x + 2) % 4, 0)
+    weight_wait(w_all, w_send, w_recv, (x + 2) % 4, 1)
+    local.wait()
+
+    def multiply(zt, target):
+        def tile(n, carry):
+            cols = pl.ds(pl.multiple_of(n * 256, 256), 256)
+            total = jnp.dot(
+                a_all[zt, 0, 0:tokens, :], w_all[0, :, cols], preferred_element_type=jnp.float32
+            )
+            for xx in range(1, 4):
+                total = total + jnp.dot(
+                    a_all[zt, xx, 0:tokens, :],
+                    w_all[xx, :, cols],
+                    preferred_element_type=jnp.float32,
+                )
+            target[:, cols] = total.astype(target.dtype)
+            return carry
+
+        lax.fori_loop(0, tiles, tile, 0)
+
+    half = tokens // 2
+    top, bottom = pl.ds(0, half), pl.ds(half, half)
+    far_up = remote(
+        product.at[0, top], relay.at[0], r_send.at[0], relay_recv.at[0], req, blk_up
+    )
+    far_down = remote(
+        product.at[0, bottom], relay.at[1], r_send.at[1], relay_recv.at[1], req, blk_down
+    )
+    up_bottom = remote(
+        product.at[1, bottom], final.at[0, bottom], r_send.at[2], final_recv.at[0, 1], req, blk_up
+    )
+    up_top = remote(
+        product.at[1, top], final.at[0, top], r_send.at[3], final_recv.at[0, 0], req, blk_up
+    )
+    down_top = remote(
+        product.at[2, top], final.at[1, top], r_send.at[4], final_recv.at[1, 0], req, blk_down
+    )
+    down_bottom = remote(
+        product.at[2, bottom], final.at[1, bottom], r_send.at[5], final_recv.at[1, 1], req, blk_down
+    )
+    multiply((zh + 2) % 4, product.at[0])
+    far_up.start()
+    far_down.start()
+    multiply((zh + 1) % 4, product.at[1])
+    up_bottom.start()
+    multiply((zh + 3) % 4, product.at[2])
+    down_top.start()
+
+    def add_relay(slot, rows, index):
+        def tile(n, carry):
+            cols = pl.ds(pl.multiple_of(n * 256, 256), 256)
+            total = product[slot, rows, cols].astype(jnp.float32) + relay[index, :, cols].astype(
+                jnp.float32
+            )
+            product[slot, rows, cols] = total.astype(jnp.bfloat16)
+            return carry
+
+        lax.fori_loop(0, tiles, tile, 0)
+
+    far_up.wait_recv()
+    add_relay(1, top, 0)
+    up_top.start()
+    far_down.wait_recv()
+    add_relay(2, bottom, 1)
+    down_bottom.start()
+    multiply(zh, own_sum)
+
+    for copy in square_copies:
+        copy.wait_recv()
+    row = square_out[zh] + square_in[0] + square_in[1] + square_in[2]
+    spread = jnp.broadcast_to(row[0:1, :], (tokens, tokens))
+    diagonal = lax.broadcasted_iota(jnp.int32, (tokens, tokens), 0) == lax.broadcasted_iota(
+        jnp.int32, (tokens, tokens), 1
+    )
+    square_sum = jnp.sum(jnp.where(diagonal, spread, 0.0), 1, keepdims=True)
+    scale = jnp.broadcast_to(lax.rsqrt(square_sum / D + EPSILON), (tokens, 128))
+
+    up_bottom.wait_recv()
+    down_top.wait_recv()
+    up_top.wait_recv()
+    down_bottom.wait_recv()
+
+    def finish(n, carry):
+        def column_sum(start):
+            cols = pl.ds(pl.multiple_of(start, 128), 128)
+            total = own_sum[:, cols] + final[0, :, cols].astype(jnp.float32)
+            return (total + final[1, :, cols].astype(jnp.float32)) * scale
+
+        gate, up = column_sum(n * 128), column_sum(width + n * 128)
+        value = gate / (1.0 + jnp.exp(-gate)) * up
+        hidden_ref[:, pl.ds(pl.multiple_of(n * 128, 128), 128)] = value.astype(jnp.bfloat16)
+        return carry
+
+    lax.fori_loop(0, width // 128, finish, 0)
+
+    for copy in sends + relays + square_copies:
+        copy.wait_send()
+    for copy in (far_up, far_down, up_bottom, up_top, down_top, down_bottom):
+        copy.wait_send()
+    drain()
+
+
+def ffn(u_ext, weights):
+    depth, wide = weights.shape
+    dma = pltpu.SemaphoreType.DMA
+    bf16, f32 = jnp.bfloat16, jnp.float32
+    return pl.pallas_call(
+        ffn_kernel,
+        out_shape=jax.ShapeDtypeStruct((128, wide // 2), bf16),
+        in_specs=[
+            pl.BlockSpec(memory_space=pltpu.VMEM),
+            pl.BlockSpec(memory_space=pl.ANY),
+        ],
+        out_specs=pl.BlockSpec(memory_space=pltpu.VMEM),
+        scratch_shapes=[
+            pltpu.VMEM((4, depth, wide), bf16),
+            pltpu.VMEM((4, 4) + u_ext.shape, bf16),
+            pltpu.VMEM((3, 128, wide), bf16),
+            pltpu.VMEM((2, 64, wide), bf16),
+            pltpu.VMEM((2, 128, wide), bf16),
+            pltpu.VMEM((128, wide), f32),
+            pltpu.VMEM((4, 8, 128), f32),
+            pltpu.VMEM((3, 8, 128), f32),
+            dma((6,)),
+            dma((4, 2)),
+            dma,
+            dma,
+            dma((4,)),
+            dma((4, 2)),
+            dma((4,)),
+            dma((4, 4)),
+            dma((4, 4)),
+            dma((6,)),
+            dma((2,)),
+            dma((2, 2)),
+            dma((3,)),
+            dma((3,)),
+        ],
+        compiler_params=pltpu.CompilerParams(collective_id=1, has_side_effects=True),
+        name="ffn",
+    )(u_ext, weights)
 
 
 def on_device(
@@ -149,21 +579,14 @@
     attention_output = (state[0] / state[2][..., None]).reshape(group_len, heads_here * head_dim)
     stream = (residual.astype(jnp.float32) + attention_output).astype(jnp.bfloat16)
     stream_f32 = stream.astype(jnp.float32)
-    square_sum = lax.psum(jnp.sum(stream_f32 * stream_f32, 1), "blk")
-    normed = (stream_f32 * lax.rsqrt(square_sum[:, None] / D + EPSILON) * gain[None, :]).astype(
-        jnp.bfloat16
-    )
-    gathered = lax.all_gather(normed, "req", axis=0, tiled=True)
+    square_sum = jnp.sum(stream_f32 * stream_f32, 1)
+    scaled = (stream_f32 * gain[None, :]).astype(jnp.bfloat16)
+    high = square_sum.astype(jnp.bfloat16)
+    low = (square_sum - high.astype(jnp.float32)).astype(jnp.bfloat16)
+    row = jnp.concatenate([high, low, jnp.zeros((gain.shape[0] - 2 * group_len,), jnp.bfloat16)])
+    u_ext = jnp.concatenate([scaled, jnp.broadcast_to(row[None, :], (16, row.shape[0]))], 0)
     weights = gate_up.reshape(gate_up.shape[0], 2 * gate_up.shape[2])
-    width_here = gate_up.shape[2]
-    summed = lax.psum_scatter(
-        jnp.dot(gathered, weights, preferred_element_type=jnp.float32).astype(jnp.bfloat16),
-        "blk",
-        scatter_dimension=0,
-        tiled=True,
-    ).astype(jnp.float32)
-    hidden = (jax.nn.silu(summed[:, :width_here]) * summed[:, width_here:]).astype(jnp.bfloat16)
-    return (hidden, updated_cache)
+    return (ffn(u_ext, weights), updated_cache)
 
 
 def solution(mesh):

time: 335 us -> 255 us (0.76); the launches traced: 334 us -> 250 us
  waiting for transfers between devices: 206 us -> 51.1 us
  Pallas kernels: 0 us -> 120 us
  blocking collectives: 40.2 us -> 0 us
  matrix products: 30.8 us -> 21.6 us
    pallas_call x0 -> x1, Pallas kernels: none -> 120 us  [ffn(): pl.pallas_call(ffn_kernel, out_shape=jax.ShapeDtypeStruct((128, wide // 2...]
    reduce_scatter x1 -> x0, waiting for transfers between devices: 114 us -> none  [on_device(): lax.psum_scatter(jnp.dot(gathered, weights, preferred_element_type=jnp.fl...]
    psum x1 -> x0, blocking collectives: 40.2 us -> none  [on_device(): square_sum = lax.psum(jnp.sum(stream_f32 * stream_f32, 1), 'blk')]
    all_gather x1 -> x0, waiting for transfers between devices: 38.1 us -> none  [on_device(): gathered = lax.all_gather(normed, 'req', axis=0, tiled=True)]
    dot_general x1 -> x0, matrix products: 9.12 us -> none  [on_device(): jnp.dot(gathered, weights, preferred_element_type=jnp.float32)]
  transfers between devices with their start and end apart: 3 -> 1, of which waited for: 3 -> 1; matrix products, arithmetic and copies ran while one was open for 2% -> 2% of each run, Pallas kernels for 0% -> 0%
where the time goes in v1:
time: 255 us; the launch traced here: 250 us
  Pallas kernels  120 us (47%)
  waiting for transfers between devices  51.1 us (20%)
  matrix products  21.6 us (8%)
  other arithmetic  21.5 us (8%)
  local copies, waits for them, and re-layouts  20 us (8%)
  between operations  15 us (6%)
    pallas_call x1, Pallas kernels, ffn(): pl.pallas_call(ffn_kernel, out_shape=jax.ShapeDtypeStruct((128, wide // 2...  120 us
    all_gather x1, waiting for transfers between devices, on_device(): shard_piece = lax.all_gather(own_slots, 'req', axis=0, tiled=True)  51.1 us
    dot_general x9, matrix products, absorb(): jnp.einsum('tqn,nd->tqd', probs.astype(jnp.bfloat16), values_in, preferre...  15.4 us
    reduce_sum x9, other arithmetic, absorb(): weight_sum = weight_sum * factor + jnp.sum(probs, -1)  12.9 us
    dynamic_slice x8, local copies, waits for them, and re-layouts, step(): lax.dynamic_slice_in_dim(pages_in, index * per_block, per_block, 0)  10.5 us
    dot_general x9, matrix products, absorb(): jnp.einsum('tqd,nd->tqn', query, keys_in, preferred_element_type=jnp.floa...  6.23 us
    lt x8, other arithmetic, step(): usable = jnp.repeat(numbers, page_len)[None, None, :] < limit  5.69 us
  transfers between devices with their start and end apart: 1, of which 1 were waited for; matrix products, arithmetic and copies ran while one was open for 2% of the time, Pallas kernels for 0%

profile of v1, /device:TPU:20, one launch (start us, length us, event | category | flops | bytes accessed | tf_op | source)
XLA Modules:
  0.0 249.9 jit_solution(4419910675856210201)
XLA Ops:
  7.3 3.4 %constant_dynamic-slice_fusion.1 = bf16[8,128,1,256]{3,2,1,0:T(2,128)(2,1)S(1)} fusion(bf16[8,128,8,256]{3,2,1,0:T(8,128)(2,1)} %param.16, s32[]{:T(128)S(6)} %select_n.68), kind=kLoop, calls=%fused_computation.66 | loop fusion | bytes 1048580 | tf_op jit(solution)/shard_map/jit(dynamic_index_in_dim)/dynamic_slice | solution.py:567
  13.7 1.6 copy.46
  17.7 51.1 %all-gather.3.cloned.1.call-done = bf16[128,128,1,256]{3,1,2,0:T(8,128)(2,1)} async-done(((bf16[8,128,1,256]{3,1,2,0:T(8,128)(2,1)}), bf16[128,128,1,256]{3,1,2,0:T(8,128)(2,1)}) %all-gather.3.cloned.1.call-update) | async-done | bytes 8388624 | tf_op jit(solution)/shard_map/all_gather | solution.py:568
  68.8 51.4 %while.17 = (s32[]{:T(128)}, f32[128,4,128]{2,0,1:T(8,128)S(1)}, f32[128,4]{0,1:T(4,128)S(1)}, f32[128,4]{0,1:T(4,128)S(1)}, s32[128]{0:T(128)S(1)}, /*index=5*/...) while((s32[]{:T(128)}, f32[128,4,128]{2,0,1:T(8,128)S(1)}, ...), condition=%wide.region_9.10_spmd, body=%wide.region_6.9_spmd.sunk | while | flops 550634496 | bytes 16427279 | solution.py:78
  69.7 1.3 constant_dynamic-slice_fusion.5
  71.7 1.6 fusion.46
  73.4 1.9 fusion.47
  76.1 1.3 constant_dynamic-slice_fusion.5
  78.2 1.6 fusion.46
  79.8 1.9 fusion.47
  84.6 1.6 fusion.46
  86.2 1.9 fusion.47
  91.0 1.6 fusion.46
  92.6 1.9 fusion.47
  97.4 1.6 fusion.46
  99.0 1.9 fusion.47
  103.8 1.6 fusion.46
  105.5 1.9 fusion.47
  110.3 1.6 fusion.46
  111.9 1.9 fusion.47
  116.7 1.6 fusion.46
  118.3 1.9 fusion.47
  121.2 120.2 %ffn.1 = bf16[128,896]{1,0:T(8,128)(2,1)} custom-call(bf16[144,512]{1,0:T(8,128)(2,1)} %pad_maximum_fusion.u_ref, bf16[512,1792]{1,0:T(8,128)(2,1)} %bitcast.73), custom_call_target="tpu_custom_call" | custom-call | tf_op jit(solution)/shard_map/ffn/pallas_call | solution.py:478
  241.4 1.6 copy.67
  (106 shorter events, 25.9 us)
Async XLA Ops:
  7.2 6.0 %copy-start = (bf16[128,8,256]{2,1,0:T(8,128)(2,1)S(1)}, bf16[128,8,256]{2,1,0:T(8,128)(2,1)}, u32[]{:S(2)}) copy-start(bf16[128,8,256]{2,1,0:T(8,128)(2,1)} %param.12) | copy-start | bytes 1572868
  7.2 4.5 %copy-start.6 = (s32[16]{0:T(128)S(1)}, s32[16]{0:T(128)}, u32[]{:S(2)}) copy-start(s32[16]{0:T(128)} %param.19) | copy-start | bytes 196
  7.2 5.7 %copy-start.4 = (s32[16,4]{0,1:T(4,128)S(1)}, s32[16,4]{0,1:T(4,128)}, u32[]{:S(2)}) copy-start(s32[16,4]{0,1:T(4,128)} %param.18) | copy-start | bytes 772
  7.2 5.9 %copy-start.3 = (bf16[128,512]{1,0:T(8,128)(2,1)S(1)}, bf16[128,512]{1,0:T(8,128)(2,1)}, u32[]{:S(2)}) copy-start(bf16[128,512]{1,0:T(8,128)(2,1)} %param.11) | copy-start | bytes 393220
  7.2 6.5 %copy-start.1 = (bf16[512,2,896]{2,1,0:T(2,128)(2,1)S(1)}, bf16[512,2,896]{2,1,0:T(2,128)(2,1)}, u32[]{:S(2)}) copy-start(bf16[512,2,896]{2,1,0:T(2,128)(2,1)} %param.15) | copy-start | bytes 5505028
  7.2 61.6 %all-gather.3.cloned.1.call-start = ((), (), s32[]{:S(2)}) async-start(), calls=%async_computation | async-start | bytes 8912896 | tf_op jit(solution)/shard_map/all_gather | solution.py:568
  10.7 6.0 %copy-start.7 = (s32[128]{0:T(128)S(1)}, s32[128]{0:T(128)}, u32[]{:S(2)}) copy-start(s32[128]{0:T(128)} %param.17) | copy-start | bytes 1540
  68.8 51.4 %copy-start.2 = (bf16[128,512]{1,0:T(8,128)(2,1)S(1)}, bf16[128,512]{1,0:T(8,128)(2,1)}, u32[]{:S(2)}) copy-start(bf16[128,512]{1,0:T(8,128)(2,1)} %param.13) | copy-start | bytes 393220
  68.8 51.4 %copy-start.5 = (f32[512]{0:T(512)S(1)}, f32[512]{0:T(512)}, u32[]{:S(2)}) copy-start(f32[512]{0:T(512)} %param.14) | copy-start | bytes 6148
Sparse Core Ops, SparseCore 0:
  11.8 57.0 all-gather.2

commit v2 on v1

--- a/solution.py
+++ b/solution.py
@@ -10,7 +10,6 @@
 D = 8192
 
 MESH = pl.DeviceIdType.MESH
-
 
 NEGATIVE = -1e30
 EPSILON = 1e-05
@@ -42,48 +41,6 @@
     )
     offset = tokens_at - request_begin
     return (request, offset, page_count * page_len + offset)
-
-
-def absorb(state, query, keys_in, values_in, usable, score_scale):
-    weighted, running_max, weight_sum = state
-    scores = (
-        jnp.einsum("tqd,nd->tqn", query, keys_in, preferred_element_type=jnp.float32) * score_scale
-    )
-    scores = jnp.where(usable, scores, NEGATIVE)
-    new_max = jnp.maximum(running_max, jnp.max(scores, -1))
-    probs = jnp.where(usable, jnp.exp(scores - new_max[..., None]), 0.0)
-    factor = jnp.exp(running_max - new_max)
-    weight_sum = weight_sum * factor + jnp.sum(probs, -1)
-    weighted = weighted * factor[..., None] + jnp.einsum(
-        "tqn,nd->tqd", probs.astype(jnp.bfloat16), values_in, preferred_element_type=jnp.float32
-    )
-    return (weighted, new_max, weight_sum)
-
-
-def absorb_pages(state, query, pages_in, page_numbers, limit, score_scale):
-    n_pages, page_len, lanes = pages_in.shape
-    head_dim = lanes // 2
-    key_target = max(page_len, (1 << 20) // (query.shape[0] * query.shape[1]))
-    per_block = math.gcd(n_pages, max(1, key_target // page_len))
-    n_blocks = n_pages // per_block
-
-    def step(index, carry):
-        block = lax.dynamic_slice_in_dim(pages_in, index * per_block, per_block, 0).reshape(
-            per_block * page_len, lanes
-        )
-        numbers = lax.dynamic_slice_in_dim(page_numbers, index * per_block, per_block, 0)
-        usable = jnp.repeat(numbers, page_len)[None, None, :] < limit
-        return absorb(carry, query, block[:, :head_dim], block[:, head_dim:], usable, score_scale)
-
-    return lax.fori_loop(0, n_blocks, step, state)
-
-
-def empty_state(rows_count, heads_here, head_dim):
-    return (
-        jnp.zeros((rows_count, heads_here, head_dim), jnp.float32),
-        jnp.full((rows_count, heads_here), NEGATIVE, jnp.float32),
-        jnp.zeros((rows_count, heads_here), jnp.float32),
-    )
 
 
 def remote(src, dst, send_sem, recv_sem, req, blk):
@@ -283,10 +240,33 @@
     return drain
 
 
-def ffn_kernel(
-    u_ref,
+def group_at(j):
+    h = j // 2
+    return h + h // 2 - 2 * (h // 3), j % 2
+
+
+def layer_kernel(
+    q_ref,
+    cos_ref,
+    sin_ref,
+    fresh_ref,
+    allowed_ref,
+    hide_ref,
+    pages_ref,
+    residual_ref,
+    gain_ref,
     w_ref,
     hidden_ref,
+    q_all,
+    kv_all,
+    values_t,
+    scores,
+    probs,
+    part_out,
+    stat_out,
+    part_in,
+    stat_in,
+    u_ref,
     w_all,
     a_all,
     product,
@@ -295,6 +275,14 @@
     own_sum,
     square_out,
     square_in,
+    query_send,
+    query_recv,
+    page_send,
+    page_recv,
+    part_send,
+    part_recv,
+    stat_send,
+    stat_recv,
     w_send,
     w_recv,
     w_local,
@@ -311,35 +299,206 @@
     q_recv,
 ):
     req, blk, y, zl, core, zh, x = place()
-    tokens, features = 128, u_ref.shape[1]
+    tokens, features = q_ref.shape
+    heads = features // 128
+    keys_here = pages_ref.shape[0]
+    rows_all = heads * tokens
     width = hidden_ref.shape[1]
     tiles = 2 * width // 256
-    over_z = y * 4 + (1 - zl) * 2 + core
     sibling = y * 4 + zl * 2 + (1 - core)
-    req_up = ((y + 1) % 4) * 4 + zl * 2 + core
-    req_down = ((y + 3) % 4) * 4 + zl * 2 + core
     blk_up, blk_far, blk_down = [((zh + i) % 4) * 4 + x for i in (1, 2, 3)]
+    turn = (1.0 / math.sqrt(128)) * math.log2(math.e)
+
+    def ahead(j):
+        dy, dz = group_at(j)
+        return ((y + dy) % 4) * 4 + ((zl + dz) % 2) * 2 + core
+
+    def behind(j):
+        dy, dz = group_at(j)
+        return ((y + 4 - dy) % 4) * 4 + ((zl + dz) % 2) * 2 + core
 
     barrier = pltpu.get_barrier_semaphore()
     peers = [(req, zh * 4 + (x + i) % 4) for i in (1, 2, 3)]
-    peers += [(over_z, blk), (sibling, blk), (req_up, blk), (req_down, blk)]
-    peers += [(req, blk_up), (req, blk_far), (req, blk_down)]
+    peers += [(sibling, blk), (req, blk_up), (req, blk_far), (req, blk_down)]
+    peers += [(ahead(j), blk) for j in range(1, 8)]
     for peer in peers:
         pl.semaphore_signal(barrier, inc=1, device_id=peer, device_id_type=MESH)
+
+    cosines, sines = cos_ref[...], sin_ref[...]
+    for h in range(heads):
+        vector = q_ref[:, h * 128 : (h + 1) * 128].astype(jnp.float32)
+        turned = vector * cosines + pltpu.roll(vector, 64, 1) * sines
+        q_all[0, h * tokens : (h + 1) * tokens, :] = turned.astype(jnp.bfloat16)
     pl.semaphore_wait(barrier, len(peers))
 
+    page_copy = remote(pages_ref, kv_all.at[core], page_send, page_recv, sibling, blk)
+    page_copy.start()
+    query_copies = [
+        remote(q_all.at[0], q_all.at[j], query_send.at[j], query_recv.at[j], ahead(j), blk)
+        for j in range(1, 8)
+    ]
+    for copy in query_copies:
+        copy.start()
     sends = weight_sends(w_ref, w_all, w_send, w_recv)
     for copy in sends:
         copy.start()
     local = pltpu.make_async_copy(w_ref, w_all.at[x], w_local)
     local.start()
-
-    drain = spread_features(u_ref, a_all, x_send, z_send, y_send, on_send, core_send, a_recv)
+    kv_all[core] = pages_ref[...]
+
+    def fold(block, op):
+        parts = [block[i * 8 : (i + 1) * 8] for i in range(block.shape[0] // 8)]
+        while len(parts) > 1:
+            parts = [op(a, b) for a, b in zip(parts[::2], parts[1::2])]
+        return parts[0]
+
+    def last_fold(rows, op):
+        return op(rows, 0, keepdims=True)
+
+    fresh_t = jnp.transpose(fresh_ref[:, 128:256].astype(jnp.float32)).astype(jnp.bfloat16)
+    raw = lax.dot_general(
+        fresh_ref[:, 0:128],
+        q_all[0],
+        (((1,), (1,)), ((), ())),
+        preferred_element_type=jnp.float32,
+    )
+    mask = jnp.concatenate([allowed_ref[...]] * heads, 1)
+    raw = jnp.where(mask > 0, raw, NEGATIVE)
+    suffix_max = last_fold(fold(raw, jnp.maximum), jnp.max)
+    suffix_probs = jnp.exp2((raw - suffix_max) * turn)
+    suffix_sum = last_fold(fold(suffix_probs, jnp.add), jnp.sum)
+    suffix_part = jnp.dot(
+        fresh_t, suffix_probs.astype(jnp.bfloat16), preferred_element_type=jnp.float32
+    )
+
+    def turn_values(which):
+        for p in range(keys_here // 128):
+            block = kv_all[which, p * 128 : (p + 1) * 128, 128:256].astype(jnp.float32)
+            where = pl.ds(pl.multiple_of(which * keys_here + p * 128, 128), 128)
+            values_t[:, where] = jnp.transpose(block).astype(jnp.bfloat16)
+
+    turn_values(core)
+    remote(pages_ref, kv_all.at[1 - core], page_send, page_recv, sibling, blk).wait_recv()
+    turn_values(1 - core)
+
+    chunk = 512
+    chunks = 2 * keys_here // chunk
+    per_core = keys_here // chunk
+
+    def score_chunk(c, j, slot, top):
+        keys = kv_all[c // per_core, (c % per_core) * chunk : (c % per_core + 1) * chunk, 0:128]
+        raw = lax.dot_general(
+            keys, q_all[j], (((1,), (1,)), ((), ())), preferred_element_type=jnp.float32
+        )
+        scores[slot, c * chunk : (c + 1) * chunk, :] = raw
+        for p in range(chunk // 128):
+            page = c * (chunk // 128) + p
+            folded = fold(raw[p * 128 : (p + 1) * 128], jnp.maximum)
+            top = jnp.maximum(top, folded + hide_ref[page, j])
+        return top
+
+    def weigh_chunk(c, j, slot, top, total, weighted):
+        for p in range(chunk // 128):
+            page = c * (chunk // 128) + p
+            rows = slice(page * 128, (page + 1) * 128)
+            level = top - 4.0 * hide_ref[page, j]
+            weights = jnp.exp2((scores[slot, rows, :] - level) * turn)
+            total = total + fold(weights, jnp.add)
+            probs[rows, :] = weights.astype(jnp.bfloat16)
+        part = jnp.dot(
+            values_t[:, c * chunk : (c + 1) * chunk],
+            probs[c * chunk : (c + 1) * chunk, :],
+            preferred_element_type=jnp.float32,
+        )
+        return total, part if weighted is None else weighted + part
+
+    def store_part(j, top, total, weighted):
+        part_out[j] = weighted.astype(jnp.bfloat16)
+        first = lax.broadcasted_iota(jnp.int32, (8, rows_all), 0) == 0
+        stat_out[j] = jnp.where(first, top, last_fold(total, jnp.sum))
+
+    def part_copies(j):
+        return (
+            remote(
+                part_out.at[j], part_in.at[j], part_send.at[j], part_recv.at[j], behind(j), blk
+            ),
+            remote(
+                stat_out.at[j], stat_in.at[j], stat_send.at[j], stat_recv.at[j], behind(j), blk
+            ),
+        )
+
+    low = jnp.full((8, rows_all), NEGATIVE, jnp.float32)
+    zero = jnp.zeros((8, rows_all), jnp.float32)
+    top = low
+    for c in range(chunks):
+        top = score_chunk(c, 0, 0, top)
+    first_top = last_fold(top, jnp.max)
+
+    def group_step(j, done_top):
+        remote(
+            q_all.at[0], q_all.at[j], query_send.at[1], query_recv.at[j], ahead(1), blk
+        ).wait_recv()
+        top, total, weighted = low, zero, None
+        for c in range(chunks):
+            top = score_chunk(c, j, j % 2, top)
+            total, weighted = weigh_chunk(c, j - 1, (j - 1) % 2, done_top, total, weighted)
+        store_part(j - 1, done_top, total, weighted)
+
+        @pl.when(j >= 2)
+        def _():
+            for copy in part_copies(j - 1):
+                copy.start()
+
+        return last_fold(top, jnp.max)
+
+    last_top = lax.fori_loop(1, 8, group_step, first_top)
+    total, weighted = zero, None
+    for c in range(chunks):
+        total, weighted = weigh_chunk(c, 7, 1, last_top, total, weighted)
+    store_part(7, last_top, total, weighted)
+    for copy in part_copies(7):
+        copy.start()
 
     relays = weight_relays(w_all, w_send, w_recv)
     for (step, part), copy in zip(((1, 0), (-1, 1)), relays):
         weight_wait(w_all, w_send, w_recv, (x + 4 - step) % 4, part)
         copy.start()
+
+    for j in range(1, 8):
+        part_copies(j)[1].wait_recv()
+    tops = [stat_out[0, 0:1, :]] + [stat_in[j, 0:1, :] for j in range(1, 8)]
+    sums = [stat_out[0, 1:2, :]] + [stat_in[j, 1:2, :] for j in range(1, 8)]
+    joint = suffix_max
+    for row in tops:
+        joint = jnp.maximum(joint, row)
+    factor = jnp.exp2((suffix_max - joint) * turn)
+    joint_sum = suffix_sum * factor
+    attended = suffix_part * factor
+    for j in range(8):
+        factor = jnp.exp2((tops[j] - joint) * turn)
+        joint_sum = joint_sum + sums[j] * factor
+        if j:
+            part_copies(j)[0].wait_recv()
+        part = part_in[j] if j else part_out[0]
+        attended = attended + part.astype(jnp.float32) * factor
+    attended = attended / joint_sum
+
+    squares_here = jnp.zeros((tokens, 128), jnp.float32)
+    for h in range(heads):
+        cols = slice(h * 128, (h + 1) * 128)
+        own = jnp.transpose(attended[:, h * tokens : (h + 1) * tokens])
+        stream = (residual_ref[:, cols].astype(jnp.float32) + own).astype(jnp.bfloat16)
+        stream = stream.astype(jnp.float32)
+        squares_here = squares_here + stream * stream
+        u_ref[0:tokens, cols] = (stream * gain_ref[:, cols]).astype(jnp.bfloat16)
+    square_row = jnp.sum(jnp.transpose(squares_here), 0, keepdims=True)
+    high = square_row.astype(jnp.bfloat16)
+    below = (square_row - high.astype(jnp.float32)).astype(jnp.bfloat16)
+    u_ref[tokens : tokens + 16, 0:128] = jnp.broadcast_to(high, (16, 128))
+    u_ref[tokens : tokens + 16, 128:256] = jnp.broadcast_to(below, (16, 128))
+    u_ref[tokens : tokens + 16, 256:features] = jnp.zeros((16, features - 256), jnp.bfloat16)
+
+    drain = spread_features(u_ref, a_all, x_send, z_send, y_send, on_send, core_send, a_recv)
 
     def squares(zt, carry):
         total = jnp.zeros((8, 128), jnp.float32)
@@ -471,27 +630,57 @@
     drain()
 
 
-def ffn(u_ext, weights):
+    for copy in query_copies:
+        copy.wait_send()
+    page_copy.wait_send()
+    for j in range(1, 8):
+        for copy in part_copies(j):
+            copy.wait_send()
+
+
+def layer(q, cosines, sines, fresh, allowed, hide, pages, residual, gain, weights):
     depth, wide = weights.shape
+    tokens, features = q.shape
+    rows_all = tokens * features // 128
+    keys = 2 * pages.shape[0]
     dma = pltpu.SemaphoreType.DMA
     bf16, f32 = jnp.bfloat16, jnp.float32
+    vmem = pl.BlockSpec(memory_space=pltpu.VMEM)
     return pl.pallas_call(
-        ffn_kernel,
-        out_shape=jax.ShapeDtypeStruct((128, wide // 2), bf16),
-        in_specs=[
-            pl.BlockSpec(memory_space=pltpu.VMEM),
-            pl.BlockSpec(memory_space=pl.ANY),
-        ],
-        out_specs=pl.BlockSpec(memory_space=pltpu.VMEM),
+        layer_kernel,
+        out_shape=jax.ShapeDtypeStruct((tokens, wide // 2), bf16),
+        in_specs=[vmem] * 5
+        + [pl.BlockSpec(memory_space=pltpu.SMEM)]
+        + [vmem] * 3
+        + [pl.BlockSpec(memory_space=pl.ANY)],
+        out_specs=vmem,
         scratch_shapes=[
+            pltpu.VMEM((8, rows_all, 128), bf16),
+            pltpu.VMEM((2,) + pages.shape, bf16),
+            pltpu.VMEM((128, keys), bf16),
+            pltpu.VMEM((2, keys, rows_all), f32),
+            pltpu.VMEM((keys, rows_all), bf16),
+            pltpu.VMEM((8, 128, rows_all), bf16),
+            pltpu.VMEM((8, 8, rows_all), f32),
+            pltpu.VMEM((8, 128, rows_all), bf16),
+            pltpu.VMEM((8, 8, rows_all), f32),
+            pltpu.VMEM((tokens + 16, features), bf16),
             pltpu.VMEM((4, depth, wide), bf16),
-            pltpu.VMEM((4, 4) + u_ext.shape, bf16),
-            pltpu.VMEM((3, 128, wide), bf16),
-            pltpu.VMEM((2, 64, wide), bf16),
-            pltpu.VMEM((2, 128, wide), bf16),
-            pltpu.VMEM((128, wide), f32),
+            pltpu.VMEM((4, 4, tokens + 16, features), bf16),
+            pltpu.VMEM((3, tokens, wide), bf16),
+            pltpu.VMEM((2, tokens // 2, wide), bf16),
+            pltpu.VMEM((2, tokens, wide), bf16),
+            pltpu.VMEM((tokens, wide), f32),
             pltpu.VMEM((4, 8, 128), f32),
             pltpu.VMEM((3, 8, 128), f32),
+            dma((8,)),
+            dma((8,)),
+            dma,
+            dma,
+            dma((8,)),
+            dma((8,)),
+            dma((8,)),
+            dma((8,)),
             dma((6,)),
             dma((4, 2)),
             dma,
@@ -508,8 +697,8 @@
             dma((3,)),
         ],
         compiler_params=pltpu.CompilerParams(collective_id=1, has_side_effects=True),
-        name="ffn",
-    )(u_ext, weights)
+        name="layer",
+    )(q, cosines, sines, fresh, allowed, hide, pages, residual, gain, weights)
 
 
 def on_device(
@@ -529,20 +718,13 @@
     group_len = queries.shape[0]
     heads_kv = suffix_key_value.shape[1]
     head_dim = suffix_key_value.shape[2] // 2
-    heads_here = queries.shape[1] // head_dim
     page_len = prefix_cache_slots.shape[1]
-    score_scale = 1.0 / math.sqrt(head_dim)
     kv_head = column * heads_kv // blocks
     page_count = counts[group_index]
     request, offset, positions = suffix_layout(
         lengths[group_index], page_count, group_len, page_len
     )
     cosines, sines = rope_tables(positions, head_dim // 2)
-    rotated_query = rotate(
-        queries.astype(jnp.float32).reshape(group_len, heads_here, head_dim),
-        cosines[:, None],
-        sines[:, None],
-    ).astype(jnp.bfloat16)
     own_head = lax.dynamic_index_in_dim(suffix_key_value, kv_head, 1, keepdims=False)
     keys_new = rotate(own_head[:, :head_dim].astype(jnp.float32), cosines, sines).astype(
         jnp.bfloat16
@@ -553,40 +735,36 @@
     updated_cache = lax.dynamic_slice_in_dim(
         both_new, column * lane_width % (2 * head_dim), lane_width, 1
     )
-    allowed = (request[:, None] == request[None, :]) & (offset[None, :] <= offset[:, None])
-    state = absorb(
-        empty_state(group_len, heads_here, head_dim),
-        rotated_query,
-        keys_new,
-        values_new,
-        allowed[:, None, :],
-        score_scale,
-    )
-    pages_total = prefix_page_slots.shape[0]
-    page_ids = jnp.arange(pages_total, dtype=jnp.int32)
+    allowed = (request[:, None] == request[None, :]) & (offset[:, None] <= offset[None, :])
     own_slots = lax.dynamic_index_in_dim(prefix_cache_slots, kv_head, 2, keepdims=False)
-    shard_piece = lax.all_gather(own_slots, "req", axis=0, tiled=True)
-    slot_ids = jnp.arange(shard_piece.shape[0], dtype=jnp.int32)
+    pages = own_slots.reshape(own_slots.shape[0] * page_len, 2 * head_dim)
+    chip_pages = 2 * own_slots.shape[0]
+    slot_ids = (group_index // 2) * chip_pages + jnp.arange(chip_pages, dtype=jnp.int32)
     match = prefix_page_slots[None, :] == slot_ids[:, None]
-    state = absorb_pages(
-        state,
-        rotated_query,
-        shard_piece,
-        jnp.sum(jnp.where(match, page_ids[None, :], 0), 1),
-        page_count,
-        score_scale,
-    )
-    attention_output = (state[0] / state[2][..., None]).reshape(group_len, heads_here * head_dim)
-    stream = (residual.astype(jnp.float32) + attention_output).astype(jnp.bfloat16)
-    stream_f32 = stream.astype(jnp.float32)
-    square_sum = jnp.sum(stream_f32 * stream_f32, 1)
-    scaled = (stream_f32 * gain[None, :]).astype(jnp.bfloat16)
-    high = square_sum.astype(jnp.bfloat16)
-    low = (square_sum - high.astype(jnp.float32)).astype(jnp.bfloat16)
-    row = jnp.concatenate([high, low, jnp.zeros((gain.shape[0] - 2 * group_len,), jnp.bfloat16)])
-    u_ext = jnp.concatenate([scaled, jnp.broadcast_to(row[None, :], (16, row.shape[0]))], 0)
-    weights = gate_up.reshape(gate_up.shape[0], 2 * gate_up.shape[2])
-    return (ffn(u_ext, weights), updated_cache)
+    page_ids = jnp.arange(prefix_page_slots.shape[0], dtype=jnp.int32)
+    page_of = jnp.sum(jnp.where(match, page_ids[None, :], 0), 1)
+    dy, dz = group_at(jnp.arange(8, dtype=jnp.int32))
+    source = (
+        ((group_index // 4 + 4 - dy) % 4) * 4
+        + ((group_index // 2 + dz) % 2) * 2
+        + group_index % 2
+    )
+    group_ids = jnp.arange(counts.shape[0], dtype=jnp.int32)
+    seen = jnp.sum(jnp.where(source[:, None] == group_ids[None, :], counts[None, :], 0), 1)
+    hide = jnp.where(page_of[:, None] < seen[None, :], 0.0, NEGATIVE).astype(jnp.float32)
+    hidden = layer(
+        queries,
+        jnp.concatenate([cosines, cosines], 1),
+        jnp.concatenate([-sines, sines], 1),
+        both_new,
+        allowed.astype(jnp.float32),
+        hide,
+        pages,
+        residual,
+        gain[None, :],
+        gate_up.reshape(gate_up.shape[0], 2 * gate_up.shape[2]),
+    )
+    return (hidden, updated_cache)
 
 
 def solution(mesh):

time: 255 us -> 138 us (0.54); the launches traced: 250 us -> 137 us
  waiting for transfers between devices: 51.1 us -> 0 us
  matrix products: 21.6 us -> 0 us
  other arithmetic: 21.5 us -> 4 us
  between operations: 15 us -> 1.45 us
  local copies, waits for them, and re-layouts: 20 us -> 8.97 us
    all_gather x1 -> x0, waiting for transfers between devices: 51.1 us -> none  [on_device(): shard_piece = lax.all_gather(own_slots, 'req', axis=0, tiled=True)]
    dot_general x18 -> x0, matrix products: 21.6 us -> none  [the longest x9 15.4 us: absorb(): jnp.einsum('tqn,nd->tqd', probs.astype(jnp.bfloat16), values_in, preferre...]
    reduce_sum x10 -> x2, other arithmetic: 13 us -> 0.36 us  [the longest x1 0.18 us: on_device(): jnp.sum(jnp.where(source[:, None] == group_ids[None, :], counts[None, :],...]
    dynamic_slice x8 -> x1, local copies, waits for them, and re-layouts: 10.5 us -> 0.62 us  [on_device(): lax.dynamic_slice_in_dim(both_new, column * lane_width % (2 * head_dim),...]
    lt x8 -> x0, other arithmetic: 5.69 us -> none  [step(): usable = jnp.repeat(numbers, page_len)[None, None, :] < limit]
  transfers between devices with their start and end apart: 1 -> 0, of which waited for: 1 -> 0; matrix products, arithmetic and copies ran while one was open for 2% -> 0% of each run, Pallas kernels for 0% -> 0%
where the time goes in v2:
time: 138 us; the launch traced here: 137 us
  Pallas kernels  122 us (88%)
  local copies, waits for them, and re-layouts  8.97 us (7%)
  other arithmetic  4 us (3%)
  between operations  1.45 us (1%)
    pallas_call x1, Pallas kernels, layer(): pl.pallas_call(layer_kernel, out_shape=jax.ShapeDtypeStruct((tokens, wide...  122 us
    unnamed x16, local copies, waits for them, and re-layouts  4.12 us
    dynamic_slice x1, local copies, waits for them, and re-layouts, on_device(): lax.dynamic_index_in_dim(prefix_cache_slots, kv_head, 2, keepdims=False)  3.42 us

profile of v2, /device:TPU:20, one launch (start us, length us, event | category | flops | bytes accessed | tf_op | source)
XLA Modules:
  0.0 136.5 jit_solution(6109319006821153242)
XLA Ops:
  0.6 0.0 copy-start
  0.6 0.0 copy-start.3
  0.7 3.4 %constant_dynamic-slice_fusion = bf16[8,128,1,256]{3,2,1,0:T(2,128)(2,1)S(1)} fusion(bf16[8,128,8,256]{3,2,1,0:T(8,128)(2,1)} %param.14, s32[]{:T(128)S(6)} %select_n.103), kind=kLoop, calls=%fused_computation.40 | loop fusion | bytes 1048580 | tf_op jit(solution)/shard_map/jit(dynamic_index_in_dim)/dynamic_slice | solution.py:739
  4.1 0.9 copy.16
  5.0 0.0 copy-done
  5.0 0.1 constant_dynamic-slice_fusion.2
  5.2 0.0 copy-done.3
  5.2 0.1 constant_dynamic-slice_fusion.3
  5.3 0.2 subtract_reduce_fusion
  5.5 0.1 convert_reduce_fusion
  5.6 0.1 select_reduce_fusion.2
  5.7 0.6 dynamic_slice.17
  7.0 0.3 fusion.4
  7.3 0.7 pad_maximum_fusion.2.fresh_ref
  8.0 0.7 pad_maximum_fusion
  8.8 0.2 select_reduce_fusion.1
  9.0 0.0 copy-done.5
  9.0 0.2 select_reduce_fusion
  9.2 0.7 compare_select_fusion.hide_ref
  9.9 0.7 and_convert_fusion.allowed_ref
  10.6 1.5 %copy.17 = bf16[64,8,2,896]{3,1,2,0:T(8,128)(2,1)} copy(bf16[64,8,2,896]{3,2,1,0:T(2,128)(2,1)S(1)} %bitcast.10) | data formatting | bytes 3670016
  12.1 122.1 %layer.1 = bf16[128,896]{1,0:T(8,128)(2,1)} custom-call(bf16[128,512]{1,0:T(8,128)(2,1)} %q_ref.1, f32[128,128]{1,0:T(8,128)} %get-tuple-element.11.cos_ref, f32[128,128]{1,0:T(8,128)} %get-tuple-element.12.sin_ref, bf16[128,256]{1,0:T(8,128)(2,1)} %pad_maximum_fusion.2.fresh_ref, f32[128,128]{1,0:T(8,128)} %and_convert_fusion.allowed_ref, ...), custom_call_target="tpu_custom_call" | custom-call | tf_op jit(solution)/shard_map/layer/pallas_call | solution.py:649
  134.2 0.6 constant_dynamic-slice_fusion.1
  134.9 1.6 %copy.21 = bf16[128,896]{1,0:T(8,128)(2,1)} copy(bf16[128,896]{1,0:T(8,128)(2,1)} %layer.1) | data formatting | bytes 458752
  (15 shorter events, 0.1 us)
Async XLA Ops:
  0.6 4.4 %copy-start = (bf16[128,8,256]{2,1,0:T(8,128)(2,1)S(1)}, bf16[128,8,256]{2,1,0:T(8,128)(2,1)}, u32[]{:S(2)}) copy-start(bf16[128,8,256]{2,1,0:T(8,128)(2,1)} %param.10) | copy-start | bytes 1572868
  0.6 4.6 %copy-start.3 = (s32[16,4]{0,1:T(4,128)S(1)}, s32[16,4]{0,1:T(4,128)}, u32[]{:S(2)}) copy-start(s32[16,4]{0,1:T(4,128)} %param.16) | copy-start | bytes 772
  0.7 5.1 %copy-start.4 = (s32[16]{0:T(128)S(1)}, s32[16]{0:T(128)}, u32[]{:S(2)}) copy-start(s32[16]{0:T(128)} %param.17) | copy-start | bytes 196
  0.7 8.3 %copy-start.5 = (s32[128]{0:T(128)S(1)}, s32[128]{0:T(128)}, u32[]{:S(2)}) copy-start(s32[128]{0:T(128)} %param.15) | copy-start | bytes 1540
  0.7 9.9 %copy-start.1 = (bf16[512,2,896]{2,1,0:T(2,128)(2,1)S(1)}, bf16[512,2,896]{2,1,0:T(2,128)(2,1)}, u32[]{:S(2)}) copy-start(bf16[512,2,896]{2,1,0:T(2,128)(2,1)} %param.13) | copy-start | bytes 5505028
  8.0 126.2 %copy-start.2 = (bf16[128,256]{1,0:T(8,128)(2,1)S(1)}, bf16[128,256]{1,0:T(8,128)(2,1)}, u32[]{:S(2)}) copy-start(bf16[128,256]{1,0:T(8,128)(2,1)} %pad_maximum_fusion.2.fresh_ref) | copy-start | bytes 196612

commit v3 on v2

--- a/solution.py
+++ b/solution.py
@@ -60,51 +60,51 @@
     return req, blk, y, zl, core, blk // 4, blk % 4
 
 
-def weight_sends(w_ref, w_all, send, recv):
+def weight_pieces(w_ref, w_all, chunk):
+    half = w_ref.shape[0] // 2
+
+    def own(part):
+        return w_ref.at[pl.ds(part * half, half), chunk]
+
+    def slot(source, part):
+        return w_all.at[source, pl.ds(part * half, half), chunk]
+
+    return own, slot
+
+
+def weight_sends(w_ref, w_all, send, recv, q, chunk):
     req, blk, y, zl, core, zh, x = place()
-    half = w_ref.shape[0] // 2
-    out = []
-    for j, (step, part) in enumerate(((1, 0), (-1, 1), (1, 1), (-1, 0))):
-        rows = pl.ds(part * half, half)
-        out.append(
-            remote(
-                w_ref.at[rows],
-                w_all.at[x, rows],
-                send.at[j],
-                recv.at[x, part],
-                req,
-                zh * 4 + (x + 4 + step) % 4,
-            )
+    own, slot = weight_pieces(w_ref, w_all, chunk)
+    return [
+        remote(
+            own(part),
+            slot(x, part),
+            send.at[j, q],
+            recv.at[x, part, q],
+            req,
+            zh * 4 + (x + 4 + step) % 4,
         )
-    return out
-
-
-def weight_relays(w_all, send, recv):
+        for j, (step, part) in enumerate(((1, 0), (-1, 1), (1, 1), (-1, 0)))
+    ]
+
+
+def weight_relays(w_ref, w_all, send, recv, q, chunk):
     req, blk, y, zl, core, zh, x = place()
-    half = w_all.shape[1] // 2
+    own, slot = weight_pieces(w_ref, w_all, chunk)
     out = []
     for j, (step, part) in enumerate(((1, 0), (-1, 1))):
         source = (x + 4 - step) % 4
-        rows = pl.ds(part * half, half)
-        piece = w_all.at[source, rows]
-        out.append(
-            remote(
-                piece,
-                piece,
-                send.at[4 + j],
-                recv.at[source, part],
-                req,
-                zh * 4 + (x + 4 + step) % 4,
-            )
-        )
+        piece = slot(source, part)
+        to_blk = zh * 4 + (x + 4 + step) % 4
+        out.append(remote(piece, piece, send.at[4 + j, q], recv.at[source, part, q], req, to_blk))
     return out
 
 
-def weight_wait(w_all, send, recv, source, part):
+def weight_wait(w_ref, w_all, send, recv, q, chunk, source, part):
     req, blk, y, zl, core, zh, x = place()
-    half = w_all.shape[1] // 2
-    piece = w_all.at[source, pl.ds(part * half, half)]
-    remote(piece, piece, send.at[0], recv.at[source, part], req, zh * 4 + (x + 1) % 4).wait_recv()
+    piece = weight_pieces(w_ref, w_all, chunk)[1](source, part)
+    to_blk = zh * 4 + (x + 1) % 4
+    remote(piece, piece, send.at[0, q], recv.at[source, part, q], req, to_blk).wait_recv()
 
 
 def spread_features(u_ref, a_all, x_send, z_send, y_send, on_send, core_send, recv):
@@ -241,8 +241,7 @@
 
 
 def group_at(j):
-    h = j // 2
-    return h + h // 2 - 2 * (h // 3), j % 2
+    return j + j // 2 - 2 * (j // 3)
 
 
 def layer_kernel(
@@ -266,6 +265,8 @@
     stat_out,
     part_in,
     stat_in,
+    held_part,
+    held_stat,
     u_ref,
     w_all,
     a_all,
@@ -309,18 +310,20 @@
     blk_up, blk_far, blk_down = [((zh + i) % 4) * 4 + x for i in (1, 2, 3)]
     turn = (1.0 / math.sqrt(128)) * math.log2(math.e)
 
+    chunks_w = (pl.ds(0, 1024), pl.ds(1024, 2 * width - 1024))
+    tiles_w = ((0, 4), (4, tiles))
+    over_z = y * 4 + (1 - zl) * 2 + core
+
     def ahead(j):
-        dy, dz = group_at(j)
-        return ((y + dy) % 4) * 4 + ((zl + dz) % 2) * 2 + core
+        return ((y + group_at(j)) % 4) * 4 + zl * 2 + core
 
     def behind(j):
-        dy, dz = group_at(j)
-        return ((y + 4 - dy) % 4) * 4 + ((zl + dz) % 2) * 2 + core
+        return ((y + 4 - group_at(j)) % 4) * 4 + zl * 2 + core
 
     barrier = pltpu.get_barrier_semaphore()
     peers = [(req, zh * 4 + (x + i) % 4) for i in (1, 2, 3)]
     peers += [(sibling, blk), (req, blk_up), (req, blk_far), (req, blk_down)]
-    peers += [(ahead(j), blk) for j in range(1, 8)]
+    peers += [(over_z, blk)] + [(ahead(j), blk) for j in range(1, 4)]
     for peer in peers:
         pl.semaphore_signal(barrier, inc=1, device_id=peer, device_id_type=MESH)
 
@@ -331,20 +334,33 @@
         q_all[0, h * tokens : (h + 1) * tokens, :] = turned.astype(jnp.bfloat16)
     pl.semaphore_wait(barrier, len(peers))
 
-    page_copy = remote(pages_ref, kv_all.at[core], page_send, page_recv, sibling, blk)
-    page_copy.start()
+    def part_of(r):
+        return ((zl + r // 2) % 2) * 2 + (core + r % 2) % 2
+
+    def page_piece(r, send, to_req):
+        piece = kv_all.at[part_of(r)]
+        return remote(piece, piece, page_send.at[send], page_recv.at[part_of(r)], to_req, blk)
+
+    own_pages = kv_all.at[part_of(0)]
+    page_copies = [
+        remote(pages_ref, own_pages, page_send.at[i], page_recv.at[part_of(0)], to_req, blk)
+        for i, to_req in enumerate((sibling, over_z))
+    ]
+    page_on = page_piece(2, 2, sibling)
     query_copies = [
         remote(q_all.at[0], q_all.at[j], query_send.at[j], query_recv.at[j], ahead(j), blk)
-        for j in range(1, 8)
+        for j in range(1, 4)
     ]
-    for copy in query_copies:
+    for copy in query_copies + page_copies:
         copy.start()
-    sends = weight_sends(w_ref, w_all, w_send, w_recv)
+    sends = []
+    for q in range(2):
+        sends += weight_sends(w_ref, w_all, w_send, w_recv, q, chunks_w[q])
     for copy in sends:
         copy.start()
     local = pltpu.make_async_copy(w_ref, w_all.at[x], w_local)
     local.start()
-    kv_all[core] = pages_ref[...]
+    kv_all[part_of(0)] = pages_ref[...]
 
     def fold(block, op):
         parts = [block[i * 8 : (i + 1) * 8] for i in range(block.shape[0] // 8)]
@@ -371,51 +387,59 @@
         fresh_t, suffix_probs.astype(jnp.bfloat16), preferred_element_type=jnp.float32
     )
 
-    def turn_values(which):
+    def turn_values(r):
         for p in range(keys_here // 128):
-            block = kv_all[which, p * 128 : (p + 1) * 128, 128:256].astype(jnp.float32)
-            where = pl.ds(pl.multiple_of(which * keys_here + p * 128, 128), 128)
-            values_t[:, where] = jnp.transpose(block).astype(jnp.bfloat16)
-
-    turn_values(core)
-    remote(pages_ref, kv_all.at[1 - core], page_send, page_recv, sibling, blk).wait_recv()
-    turn_values(1 - core)
+            block = kv_all[part_of(r), p * 128 : (p + 1) * 128, 128:256].astype(jnp.float32)
+            start = r * keys_here + p * 128
+            values_t[:, start : start + 128] = jnp.transpose(block).astype(jnp.bfloat16)
+
+    turn_values(0)
+    page_piece(1, 2, sibling).wait_recv()
+    turn_values(1)
 
     chunk = 512
     chunks = 2 * keys_here // chunk
     per_core = keys_here // chunk
-
-    def score_chunk(c, j, slot, top):
-        keys = kv_all[c // per_core, (c % per_core) * chunk : (c % per_core + 1) * chunk, 0:128]
+    pages_per_core = keys_here // 128
+
+    def score_chunk(c, j, a, slot, top):
+        part = part_of(2 * a + c // per_core)
+        inside = c % per_core
+        keys = kv_all[part, inside * chunk : (inside + 1) * chunk, 0:128]
         raw = lax.dot_general(
             keys, q_all[j], (((1,), (1,)), ((), ())), preferred_element_type=jnp.float32
         )
         scores[slot, c * chunk : (c + 1) * chunk, :] = raw
         for p in range(chunk // 128):
-            page = c * (chunk // 128) + p
+            page = part * pages_per_core + inside * (chunk // 128) + p
             folded = fold(raw[p * 128 : (p + 1) * 128], jnp.maximum)
             top = jnp.maximum(top, folded + hide_ref[page, j])
         return top
 
-    def weigh_chunk(c, j, slot, top, total, weighted):
+    def weigh_chunk(c, j, a, slot, top, total, weighted):
+        part = part_of(2 * a + c // per_core)
         for p in range(chunk // 128):
-            page = c * (chunk // 128) + p
-            rows = slice(page * 128, (page + 1) * 128)
+            page = part * pages_per_core + (c % per_core) * (chunk // 128) + p
+            rows = slice(c * chunk + p * 128, c * chunk + (p + 1) * 128)
             level = top - 4.0 * hide_ref[page, j]
             weights = jnp.exp2((scores[slot, rows, :] - level) * turn)
             total = total + fold(weights, jnp.add)
             probs[rows, :] = weights.astype(jnp.bfloat16)
-        part = jnp.dot(
-            values_t[:, c * chunk : (c + 1) * chunk],
+        columns = pl.ds(pl.multiple_of(a * 2 * keys_here + c * chunk, chunk), chunk)
+        product_here = jnp.dot(
+            values_t[:, columns],
             probs[c * chunk : (c + 1) * chunk, :],
             preferred_element_type=jnp.float32,
         )
-        return total, part if weighted is None else weighted + part
-
-    def store_part(j, top, total, weighted):
-        part_out[j] = weighted.astype(jnp.bfloat16)
-        first = lax.broadcasted_iota(jnp.int32, (8, rows_all), 0) == 0
-        stat_out[j] = jnp.where(first, top, last_fold(total, jnp.sum))
+        return total, product_here if weighted is None else weighted + product_here
+
+    first_row = lax.broadcasted_iota(jnp.int32, (8, rows_all), 0) == 0
+
+    def merge(j, top, total, weighted):
+        other_top, other_sum = held_stat[j, 0:1, :], held_stat[j, 1:2, :]
+        joint = jnp.maximum(top, other_top)
+        here, there = jnp.exp2((top - joint) * turn), jnp.exp2((other_top - joint) * turn)
+        return joint, total * here + other_sum * there, weighted * here + held_part[j] * there
 
     def part_copies(j):
         return (
@@ -427,60 +451,96 @@
             ),
         )
 
+    def unit(u):
+        v = u - 4
+        later = jnp.where(v == 0, 3, jnp.where(v == 3, 0, v))
+        return jnp.where(u < 4, u, later), jnp.where(u < 4, 0, 1)
+
     low = jnp.full((8, rows_all), NEGATIVE, jnp.float32)
     zero = jnp.zeros((8, rows_all), jnp.float32)
     top = low
     for c in range(chunks):
-        top = score_chunk(c, 0, 0, top)
+        top = score_chunk(c, 0, 0, 0, top)
     first_top = last_fold(top, jnp.max)
 
-    def group_step(j, done_top):
-        remote(
-            q_all.at[0], q_all.at[j], query_send.at[1], query_recv.at[j], ahead(1), blk
-        ).wait_recv()
+    def unit_step(u, done_top):
+        j, a = unit(u)
+        before, before_half = unit(u - 1)
+
+        @pl.when(u < 4)
+        def _():
+            remote(
+                q_all.at[0], q_all.at[j], query_send.at[1], query_recv.at[j], ahead(1), blk
+            ).wait_recv()
+
+        @pl.when(u == 3)
+        def _():
+            page_piece(2, 2, over_z).wait_recv()
+            page_on.start()
+            turn_values(2)
+
+        @pl.when(u == 4)
+        def _():
+            page_piece(3, 2, sibling).wait_recv()
+            turn_values(3)
+
         top, total, weighted = low, zero, None
         for c in range(chunks):
-            top = score_chunk(c, j, j % 2, top)
-            total, weighted = weigh_chunk(c, j - 1, (j - 1) % 2, done_top, total, weighted)
-        store_part(j - 1, done_top, total, weighted)
-
-        @pl.when(j >= 2)
+            top = score_chunk(c, j, a, u % 2, top)
+            total, weighted = weigh_chunk(
+                c, before, before_half, (u - 1) % 2, done_top, total, weighted
+            )
+        total = last_fold(total, jnp.sum)
+
+        @pl.when(u <= 4)
         def _():
-            for copy in part_copies(j - 1):
+            held_part[before] = weighted
+            held_stat[before] = jnp.where(first_row, done_top, total)
+
+        @pl.when(u > 4)
+        def _():
+            joint, joint_sum, joint_part = merge(before, done_top, total, weighted)
+            part_out[before] = joint_part.astype(jnp.bfloat16)
+            stat_out[before] = jnp.where(first_row, joint, joint_sum)
+            for copy in part_copies(before):
                 copy.start()
 
         return last_fold(top, jnp.max)
 
-    last_top = lax.fori_loop(1, 8, group_step, first_top)
+    last_top = lax.fori_loop(1, 8, unit_step, first_top)
+
+    relays = []
+
+    def relay_chunk(q):
+        copies = weight_relays(w_ref, w_all, w_send, w_recv, q, chunks_w[q])
+        for (step, part), copy in zip(((1, 0), (-1, 1)), copies):
+            source = (x + 4 - step) % 4
+            weight_wait(w_ref, w_all, w_send, w_recv, q, chunks_w[q], source, part)
+            copy.start()
+        relays.extend(copies)
+
+    relay_chunk(0)
     total, weighted = zero, None
     for c in range(chunks):
-        total, weighted = weigh_chunk(c, 7, 1, last_top, total, weighted)
-    store_part(7, last_top, total, weighted)
-    for copy in part_copies(7):
-        copy.start()
-
-    relays = weight_relays(w_all, w_send, w_recv)
-    for (step, part), copy in zip(((1, 0), (-1, 1)), relays):
-        weight_wait(w_all, w_send, w_recv, (x + 4 - step) % 4, part)
-        copy.start()
-
-    for j in range(1, 8):
+        total, weighted = weigh_chunk(c, 0, 1, 1, last_top, total, weighted)
+    own_top, own_total, own_part = merge(0, last_top, last_fold(total, jnp.sum), weighted)
+
+    order = (1, 2, 3)
+    for j in order:
         part_copies(j)[1].wait_recv()
-    tops = [stat_out[0, 0:1, :]] + [stat_in[j, 0:1, :] for j in range(1, 8)]
-    sums = [stat_out[0, 1:2, :]] + [stat_in[j, 1:2, :] for j in range(1, 8)]
-    joint = suffix_max
+    tops = [stat_in[j, 0:1, :] for j in order]
+    sums = [stat_in[j, 1:2, :] for j in order]
+    joint = jnp.maximum(suffix_max, own_top)
     for row in tops:
         joint = jnp.maximum(joint, row)
-    factor = jnp.exp2((suffix_max - joint) * turn)
-    joint_sum = suffix_sum * factor
-    attended = suffix_part * factor
-    for j in range(8):
-        factor = jnp.exp2((tops[j] - joint) * turn)
-        joint_sum = joint_sum + sums[j] * factor
-        if j:
-            part_copies(j)[0].wait_recv()
-        part = part_in[j] if j else part_out[0]
-        attended = attended + part.astype(jnp.float32) * factor
+    factor, own_factor = (jnp.exp2((row - joint) * turn) for row in (suffix_max, own_top))
+    joint_sum = suffix_sum * factor + own_total * own_factor
+    attended = suffix_part * factor + own_part * own_factor
+    for j, row, row_sum in zip(order, tops, sums):
+        factor = jnp.exp2((row - joint) * turn)
+        joint_sum = joint_sum + row_sum * factor
+        part_copies(j)[0].wait_recv()
+        attended = attended + part_in[j].astype(jnp.float32) * factor
     attended = attended / joint_sum
 
     squares_here = jnp.zeros((tokens, 128), jnp.float32)
@@ -498,6 +558,7 @@
     u_ref[tokens : tokens + 16, 128:256] = jnp.broadcast_to(below, (16, 128))
     u_ref[tokens : tokens + 16, 256:features] = jnp.zeros((16, features - 256), jnp.bfloat16)
 
+    relay_chunk(1)
     drain = spread_features(u_ref, a_all, x_send, z_send, y_send, on_send, core_send, a_recv)
 
     def squares(zt, carry):
@@ -525,13 +586,7 @@
     for copy in square_copies:
         copy.start()
 
-    weight_wait(w_all, w_send, w_recv, (x + 3) % 4, 1)
-    weight_wait(w_all, w_send, w_recv, (x + 1) % 4, 0)
-    weight_wait(w_all, w_send, w_recv, (x + 2) % 4, 0)
-    weight_wait(w_all, w_send, w_recv, (x + 2) % 4, 1)
-    local.wait()
-
-    def multiply(zt, target):
+    def multiply(zt, target, q):
         def tile(n, carry):
             cols = pl.ds(pl.multiple_of(n * 256, 256), 256)
             total = jnp.dot(
@@ -546,37 +601,39 @@
             target[:, cols] = total.astype(target.dtype)
             return carry
 
-        lax.fori_loop(0, tiles, tile, 0)
+        lax.fori_loop(*tiles_w[q], tile, 0)
 
     half = tokens // 2
-    top, bottom = pl.ds(0, half), pl.ds(half, half)
-    far_up = remote(
-        product.at[0, top], relay.at[0], r_send.at[0], relay_recv.at[0], req, blk_up
-    )
-    far_down = remote(
-        product.at[0, bottom], relay.at[1], r_send.at[1], relay_recv.at[1], req, blk_down
-    )
-    up_bottom = remote(
-        product.at[1, bottom], final.at[0, bottom], r_send.at[2], final_recv.at[0, 1], req, blk_up
-    )
-    up_top = remote(
-        product.at[1, top], final.at[0, top], r_send.at[3], final_recv.at[0, 0], req, blk_up
-    )
-    down_top = remote(
-        product.at[2, top], final.at[1, top], r_send.at[4], final_recv.at[1, 0], req, blk_down
-    )
-    down_bottom = remote(
-        product.at[2, bottom], final.at[1, bottom], r_send.at[5], final_recv.at[1, 1], req, blk_down
-    )
-    multiply((zh + 2) % 4, product.at[0])
-    far_up.start()
-    far_down.start()
-    multiply((zh + 1) % 4, product.at[1])
-    up_bottom.start()
-    multiply((zh + 3) % 4, product.at[2])
-    down_top.start()
-
-    def add_relay(slot, rows, index):
+    top_rows, bottom_rows = pl.ds(0, half), pl.ds(half, half)
+
+    def exchange(q):
+        cols = chunks_w[q]
+
+        def piece(i, slot, rows, target, recv, to_blk):
+            source = product.at[slot, rows, cols]
+            return remote(source, target, r_send.at[i, q], recv, req, to_blk)
+
+        def landing(side, rows):
+            return final.at[side, rows, cols]
+
+        return (
+            piece(0, 0, top_rows, relay.at[0, :, cols], relay_recv.at[0, q], blk_up),
+            piece(1, 0, bottom_rows, relay.at[1, :, cols], relay_recv.at[1, q], blk_down),
+            piece(2, 1, bottom_rows, landing(0, bottom_rows), final_recv.at[0, 1, q], blk_up),
+            piece(3, 2, top_rows, landing(1, top_rows), final_recv.at[1, 0, q], blk_down),
+            piece(4, 1, top_rows, landing(0, top_rows), final_recv.at[0, 0, q], blk_up),
+            piece(5, 2, bottom_rows, landing(1, bottom_rows), final_recv.at[1, 1, q], blk_down),
+        )
+
+    exchanges = [exchange(0), exchange(1)]
+
+    def wait_weights(q):
+        for step, part in ((3, 0), (3, 1), (1, 0), (1, 1), (2, 0), (2, 1)):
+            if (step, part) not in ((3, 0), (1, 1)):
+                source = (x + step) % 4
+                weight_wait(w_ref, w_all, w_send, w_recv, q, chunks_w[q], source, part)
+
+    def add_relay(slot, rows, index, q):
         def tile(n, carry):
             cols = pl.ds(pl.multiple_of(n * 256, 256), 256)
             total = product[slot, rows, cols].astype(jnp.float32) + relay[index, :, cols].astype(
@@ -585,15 +642,37 @@
             product[slot, rows, cols] = total.astype(jnp.bfloat16)
             return carry
 
-        lax.fori_loop(0, tiles, tile, 0)
-
-    far_up.wait_recv()
-    add_relay(1, top, 0)
-    up_top.start()
-    far_down.wait_recv()
-    add_relay(2, bottom, 1)
-    down_bottom.start()
-    multiply(zh, own_sum)
+        lax.fori_loop(*tiles_w[q], tile, 0)
+
+    def send_far(q):
+        wait_weights(q)
+        multiply((zh + 2) % 4, product.at[0], q)
+        exchanges[q][0].start()
+        exchanges[q][1].start()
+
+    def send_near(q):
+        multiply((zh + 1) % 4, product.at[1], q)
+        exchanges[q][2].start()
+        multiply((zh + 3) % 4, product.at[2], q)
+        exchanges[q][3].start()
+
+    def send_sums(q):
+        exchanges[q][0].wait_recv()
+        add_relay(1, top_rows, 0, q)
+        exchanges[q][4].start()
+        exchanges[q][1].wait_recv()
+        add_relay(2, bottom_rows, 1, q)
+        exchanges[q][5].start()
+
+    local.wait()
+    send_far(0)
+    send_near(0)
+    send_far(1)
+    send_sums(0)
+    send_near(1)
+    send_sums(1)
+    multiply(zh, own_sum, 0)
+    multiply(zh, own_sum, 1)
 
     for copy in square_copies:
         copy.wait_recv()
@@ -605,35 +684,31 @@
     square_sum = jnp.sum(jnp.where(diagonal, spread, 0.0), 1, keepdims=True)
     scale = jnp.broadcast_to(lax.rsqrt(square_sum / D + EPSILON), (tokens, 128))
 
-    up_bottom.wait_recv()
-    down_top.wait_recv()
-    up_top.wait_recv()
-    down_bottom.wait_recv()
-
     def finish(n, carry):
         def column_sum(start):
             cols = pl.ds(pl.multiple_of(start, 128), 128)
             total = own_sum[:, cols] + final[0, :, cols].astype(jnp.float32)
             return (total + final[1, :, cols].astype(jnp.float32)) * scale
 
-        gate, up = column_sum(n * 128), column_sum(width + n * 128)
+        gate, up = column_sum(n * 256), column_sum(n * 256 + 128)
         value = gate / (1.0 + jnp.exp(-gate)) * up
         hidden_ref[:, pl.ds(pl.multiple_of(n * 128, 128), 128)] = value.astype(jnp.bfloat16)
         return carry
 
-    lax.fori_loop(0, width // 128, finish, 0)
+    for q in range(2):
+        for copy in exchanges[q][2:]:
+            copy.wait_recv()
+        lax.fori_loop(*tiles_w[q], finish, 0)
 
     for copy in sends + relays + square_copies:
         copy.wait_send()
-    for copy in (far_up, far_down, up_bottom, up_top, down_top, down_bottom):
+    for q in range(2):
+        for copy in exchanges[q]:
+            copy.wait_send()
+    drain()
+    for copy in query_copies + page_copies + [page_on]:
         copy.wait_send()
-    drain()
-
-
-    for copy in query_copies:
-        copy.wait_send()
-    page_copy.wait_send()
-    for j in range(1, 8):
+    for j in order:
         for copy in part_copies(j):
             copy.wait_send()
 
@@ -643,6 +718,7 @@
     tokens, features = q.shape
     rows_all = tokens * features // 128
     keys = 2 * pages.shape[0]
+    groups = 4
     dma = pltpu.SemaphoreType.DMA
     bf16, f32 = jnp.bfloat16, jnp.float32
     vmem = pl.BlockSpec(memory_space=pltpu.VMEM)
@@ -655,15 +731,17 @@
         + [pl.BlockSpec(memory_space=pl.ANY)],
         out_specs=vmem,
         scratch_shapes=[
-            pltpu.VMEM((8, rows_all, 128), bf16),
-            pltpu.VMEM((2,) + pages.shape, bf16),
-            pltpu.VMEM((128, keys), bf16),
+            pltpu.VMEM((groups, rows_all, 128), bf16),
+            pltpu.VMEM((4,) + pages.shape, bf16),
+            pltpu.VMEM((128, 2 * keys), bf16),
             pltpu.VMEM((2, keys, rows_all), f32),
             pltpu.VMEM((keys, rows_all), bf16),
-            pltpu.VMEM((8, 128, rows_all), bf16),
-            pltpu.VMEM((8, 8, rows_all), f32),
-            pltpu.VMEM((8, 128, rows_all), bf16),
-            pltpu.VMEM((8, 8, rows_all), f32),
+            pltpu.VMEM((groups, 128, rows_all), bf16),
+            pltpu.VMEM((groups, 8, rows_all), f32),
+            pltpu.VMEM((groups, 128, rows_all), bf16),
+            pltpu.VMEM((groups, 8, rows_all), f32),
+            pltpu.VMEM((groups, 128, rows_all), f32),
+            pltpu.VMEM((groups, 8, rows_all), f32),
             pltpu.VMEM((tokens + 16, features), bf16),
             pltpu.VMEM((4, depth, wide), bf16),
             pltpu.VMEM((4, 4, tokens + 16, features), bf16),
@@ -673,16 +751,16 @@
             pltpu.VMEM((tokens, wide), f32),
             pltpu.VMEM((4, 8, 128), f32),
             pltpu.VMEM((3, 8, 128), f32),
-            dma((8,)),
-            dma((8,)),
-            dma,
-            dma,
-            dma((8,)),
-            dma((8,)),
-            dma((8,)),
-            dma((8,)),
-            dma((6,)),
-            dma((4, 2)),
+            dma((groups,)),
+            dma((groups,)),
+            dma((3,)),
+            dma((4,)),
+            dma((groups,)),
+            dma((groups,)),
+            dma((groups,)),
+            dma((groups,)),
+            dma((6, 2)),
+            dma((4, 2, 2)),
             dma,
             dma,
             dma((4,)),
@@ -690,9 +768,9 @@
             dma((4,)),
             dma((4, 4)),
             dma((4, 4)),
-            dma((6,)),
-            dma((2,)),
+            dma((6, 2)),
             dma((2, 2)),
+            dma((2, 2, 2)),
             dma((3,)),
             dma((3,)),
         ],
@@ -738,20 +816,19 @@
     allowed = (request[:, None] == request[None, :]) & (offset[:, None] <= offset[None, :])
     own_slots = lax.dynamic_index_in_dim(prefix_cache_slots, kv_head, 2, keepdims=False)
     pages = own_slots.reshape(own_slots.shape[0] * page_len, 2 * head_dim)
-    chip_pages = 2 * own_slots.shape[0]
-    slot_ids = (group_index // 2) * chip_pages + jnp.arange(chip_pages, dtype=jnp.int32)
+    near_pages = 4 * own_slots.shape[0]
+    slot_ids = (group_index // 4) * near_pages + jnp.arange(near_pages, dtype=jnp.int32)
     match = prefix_page_slots[None, :] == slot_ids[:, None]
     page_ids = jnp.arange(prefix_page_slots.shape[0], dtype=jnp.int32)
     page_of = jnp.sum(jnp.where(match, page_ids[None, :], 0), 1)
-    dy, dz = group_at(jnp.arange(8, dtype=jnp.int32))
-    source = (
-        ((group_index // 4 + 4 - dy) % 4) * 4
-        + ((group_index // 2 + dz) % 2) * 2
-        + group_index % 2
-    )
+    dy = group_at(jnp.arange(4, dtype=jnp.int32))
+    source = ((group_index // 4 + 4 - dy) % 4) * 4 + group_index % 4
     group_ids = jnp.arange(counts.shape[0], dtype=jnp.int32)
     seen = jnp.sum(jnp.where(source[:, None] == group_ids[None, :], counts[None, :], 0), 1)
     hide = jnp.where(page_of[:, None] < seen[None, :], 0.0, NEGATIVE).astype(jnp.float32)
+    depth, _, width = gate_up.shape
+    weights = gate_up.reshape(depth, 2, width // 128, 128).transpose(0, 2, 1, 3)
+    weights = weights.reshape(depth, 2 * width)
     hidden = layer(
         queries,
         jnp.concatenate([cosines, cosines], 1),
@@ -762,7 +839,7 @@
         pages,
         residual,
         gain[None, :],
-        gate_up.reshape(gate_up.shape[0], 2 * gate_up.shape[2]),
+        weights,
     )
     return (hidden, updated_cache)
 

time: 138 us -> 146 us (1.058)
  local copies, waits for them, and re-layouts: 8.97 us -> 18.5 us
    transpose x0 -> x1, local copies, waits for them, and re-layouts: none -> 5.21 us  [on_device(): weights = gate_up.reshape(depth, 2, width // 128, 128).transpose(0, 2, 1, 3)]
    unnamed x16, local copies, waits for them, and re-layouts: 4.12 us -> 6.82 us
    reshape x0 -> x1, local copies, waits for them, and re-layouts: none -> 1.76 us  [on_device(): weights = weights.reshape(depth, 2 * width)]
where the time goes in v3:
time: 146 us; the launch traced here: 145 us
  Pallas kernels  121 us (83%)
  local copies, waits for them, and re-layouts  18.5 us (13%)
  other arithmetic  4 us (3%)
  between operations  1.46 us (1%)
    pallas_call x1, Pallas kernels, layer(): pl.pallas_call(layer_kernel, out_shape=jax.ShapeDtypeStruct((tokens, wide...  121 us
    unnamed x16, local copies, waits for them, and re-layouts  6.82 us
    transpose x1, local copies, waits for them, and re-layouts, on_device(): weights = gate_up.reshape(depth, 2, width // 128, 128).transpose(0, 2, 1, 3)  5.21 us
    dynamic_slice x1, local copies, waits for them, and re-layouts, on_device(): lax.dynamic_index_in_dim(prefix_cache_slots, kv_head, 2, keepdims=False)  3.32 us

profile of v3, /device:TPU:20, one launch (start us, length us, event | category | flops | bytes accessed | tf_op | source)
XLA Modules:
  0.0 144.8 jit_solution(4557879826684872467)
XLA Ops:
  0.6 0.0 copy-start
  0.7 3.3 %constant_dynamic-slice_fusion = bf16[8,128,1,256]{3,2,1,0:T(2,128)(2,1)S(1)} fusion(bf16[8,128,8,256]{3,2,1,0:T(8,128)(2,1)} %param.14, s32[]{:T(128)S(6)} %select_n.77), kind=kLoop, calls=%fused_computation.35 | loop fusion | bytes 1048580 | tf_op jit(solution)/shard_map/jit(dynamic_index_in_dim)/dynamic_slice | solution.py:817
  4.0 0.0 copy-start.5
  4.0 0.0 copy-start.1
  4.0 0.9 copy.21
  4.9 0.1 constant_dynamic-slice_fusion.2
  5.1 0.1 constant_dynamic-slice_fusion.3
  5.2 0.2 subtract_reduce_fusion
  5.4 0.1 convert_reduce_fusion
  5.5 0.1 select_reduce_fusion.2
  5.6 0.6 dynamic_slice.17
  6.9 0.3 fusion.4
  7.2 0.7 pad_maximum_fusion.2.fresh_ref
  7.9 0.7 pad_maximum_fusion
  8.7 0.2 select_reduce_fusion.1
  8.9 0.2 select_reduce_fusion
  9.1 0.7 compare_select_fusion.hide_ref
  9.8 0.7 and_convert_fusion.allowed_ref
  10.5 4.2 %copy.18 = bf16[512,2,896]{0,2,1:T(8,128)(2,1)} copy(bf16[512,2,896]{2,1,0:T(2,128)(2,1)S(1)} %copy-done.1) | data formatting | bytes 3670016 | tf_op args[4]
  14.7 5.2 %copy.19 = bf16[512,7,2,128]{3,2,1,0:T(2,128)(2,1)S(1)} copy(bf16[512,7,2,128]{0,3,1,2:T(8,128)(2,1)} %bitcast.9) | data formatting | bytes 3670016 | tf_op jit(solution)/shard_map/transpose | solution.py:830
  19.9 1.8 %reshape.100.w_ref = bf16[512,1792]{1,0:T(8,128)(2,1)} reshape(bf16[512,7,2,128]{3,2,1,0:T(2,128)(2,1)S(1)} %copy.19) | data formatting | bytes 3670016 | tf_op jit(solution)/shard_map/reshape | solution.py:831
  21.7 120.8 %layer.1 = bf16[128,896]{1,0:T(8,128)(2,1)} custom-call(bf16[128,512]{1,0:T(8,128)(2,1)} %q_ref.1, f32[128,128]{1,0:T(8,128)} %get-tuple-element.11.cos_ref, f32[128,128]{1,0:T(8,128)} %get-tuple-element.12.sin_ref, bf16[128,256]{1,0:T(8,128)(2,1)} %pad_maximum_fusion.2.fresh_ref, f32[128,128]{1,0:T(8,128)} %and_convert_fusion.allowed_ref, ...), custom_call_target="tpu_custom_call" | custom-call | tf_op jit(solution)/shard_map/layer/pallas_call | solution.py:725
  142.6 0.6 constant_dynamic-slice_fusion.1
  143.2 1.6 %copy.25 = bf16[128,896]{1,0:T(8,128)(2,1)} copy(bf16[128,896]{1,0:T(8,128)(2,1)} %layer.1) | data formatting | bytes 458752
  (17 shorter events, 0.1 us)
Async XLA Ops:
  0.6 4.3 %copy-start = (bf16[128,8,256]{2,1,0:T(8,128)(2,1)S(1)}, bf16[128,8,256]{2,1,0:T(8,128)(2,1)}, u32[]{:S(2)}) copy-start(bf16[128,8,256]{2,1,0:T(8,128)(2,1)} %param.10) | copy-start | bytes 1572868
  0.7 4.5 %copy-start.3 = (s32[16,4]{0,1:T(4,128)S(1)}, s32[16,4]{0,1:T(4,128)}, u32[]{:S(2)}) copy-start(s32[16,4]{0,1:T(4,128)} %param.16) | copy-start | bytes 772
  0.7 4.9 %copy-start.4 = (s32[16]{0:T(128)S(1)}, s32[16]{0:T(128)}, u32[]{:S(2)}) copy-start(s32[16]{0:T(128)} %param.17) | copy-start | bytes 196
  4.0 4.9 %copy-start.5 = (s32[128]{0:T(128)S(1)}, s32[128]{0:T(128)}, u32[]{:S(2)}) copy-start(s32[128]{0:T(128)} %param.15) | copy-start | bytes 1540
  4.0 6.5 %copy-start.1 = (bf16[512,2,896]{2,1,0:T(2,128)(2,1)S(1)}, bf16[512,2,896]{2,1,0:T(2,128)(2,1)}, u32[]{:S(2)}) copy-start(bf16[512,2,896]{2,1,0:T(2,128)(2,1)} %param.13) | copy-start | bytes 5505028
  21.7 120.9 %copy-start.2 = (bf16[128,256]{1,0:T(8,128)(2,1)S(1)}, bf16[128,256]{1,0:T(8,128)(2,1)}, u32[]{:S(2)}) copy-start(bf16[128,256]{1,0:T(8,128)(2,1)} %pad_maximum_fusion.2.fresh_ref) | copy-start | bytes 196612
